TPU v7x, 32 devices: a whole 2x2x4 slice. The times are simulated.
32 devices in a mesh: dp: 16 (over z, y, x), tensor: 2 (over core).
Axes of the slice: x: 2, y: 2, z: 4, core: 2. Of those that a mesh axis runs over, the one named last changes fastest.
Arguments:
- layer_in: bfloat16 [16384, 1024], P(('dp', 'tensor')), may hold values from -6 to 6
- w_qkv: bfloat16 [3, 1024, 1024], P(None, 'dp', 'tensor'), may hold values from -1 to 1
- b_qv: bfloat16 [2, 16, 64], P(None, 'tensor', 'dp'), may hold values from -3 to 3
- w_proj: bfloat16 [1024, 1024], P('tensor', 'dp'), may hold values from -0.5 to 0.5
- w_ff1: bfloat16 [1024, 4096], P('dp', 'tensor'), may hold values from -0.1875 to 0.1875
- b_ff1: bfloat16 [64, 64], P('tensor', 'dp'), may hold values from -3 to 3
- w_ff2: bfloat16 [4096, 1024], P('tensor', 'dp'), may hold values from -0.09375 to 0.09375
- norm_gains: float32 [2, 1024], P(None, ('dp', 'tensor')), may hold values from 0.5 to 1.5
- add_biases: float32 [4, 1024], P(None, ('dp', 'tensor')), may hold values from -3 to 3
- cotangent: bfloat16 [16384, 1024], P(('dp', 'tensor')), may hold values from -6 to 6
Outputs:
- layer_out: bfloat16 [16384, 1024], P(('dp', 'tensor'))
- grad_in: float32 [16384, 1024], P(('dp', 'tensor'))
- grad_w_qkv: float32 [3, 1024, 1024], P(None, 'dp', 'tensor')
- grad_b_qv: float32 [2, 16, 64], P(None, 'tensor', 'dp')
- grad_w_proj: float32 [1024, 1024], P('tensor', 'dp')
- grad_w_ff1: float32 [1024, 4096], P('dp', 'tensor')
- grad_b_ff1: float32 [64, 64], P('tensor', 'dp')
- grad_w_ff2: float32 [4096, 1024], P('tensor', 'dp')
- grad_gains: float32 [2, 1024], P(None, ('dp', 'tensor'))
- grad_biases: float32 [4, 1024], P(None, ('dp', 'tensor'))
All inputs are finite; a program needn't handle non-finite values.
Results may differ from a plain program's by a relative error of at most 0.015.
Values may be sent and summed in bfloat16 or wider, within the bound.
A program may use at most 192 MiB of HBM per device.

v0:
```python
import functools
import math
import jax
import jax.numpy as jnp
from jax import lax
from jax.experimental import pallas as pl
from jax.experimental.pallas import tpu as pltpu
from jax.sharding import PartitionSpec as P

MESH = pl.DeviceIdType.MESH
ANY = pl.BlockSpec(memory_space=pl.ANY)
VM = pl.BlockSpec(memory_space=pltpu.VMEM)


def bits_of(index, count):
    return [lax.rem(index // (1 << b), 2) for b in range(count)]


def partner_of(index, mine, b):
    return index + (1 - 2 * mine[b]) * (1 << b)


def halving_orders(count):
    return [[(start + i) % count for i in range(count)] for start in range(3)]


def enter(index, mine, count, other):
    barrier = pltpu.get_barrier_semaphore()
    for b in range(count):
        pl.semaphore_signal(barrier, inc=1, device_id={"dp": partner_of(index, mine, b)}, device_id_type=MESH)
    pl.semaphore_signal(barrier, inc=1, device_id={"tensor": other}, device_id_type=MESH)
    pl.semaphore_wait(barrier, count + 1)


def block_index(mine, held, count):
    return tuple(slice(None) if b in held else mine[b] for b in reversed(range(count)))

SEQ_LEN = 1024
HD = 64
H = 16
epsilon = 1e-05
gelu_scale = 0.7978845608028654
F32 = jnp.float32
BF = jnp.bfloat16
TILE = 512
QB = 256
GATHER_MODES = (0, 1, 0, 1, 0, 1, 0, 2)
GATHER_LOOK = 4


def dot_nn(a, b):
    return lax.dot_general(a, b, (((1,), (0,)), ((), ())), preferred_element_type=F32)


def dot_nt(a, b):
    return lax.dot_general(a, b, (((1,), (1,)), ((), ())), preferred_element_type=F32)


def dot_tn(a, b):
    return lax.dot_general(a, b, (((0,), (0,)), ((), ())), preferred_element_type=F32)


def span(i, size):
    return pl.ds(pl.multiple_of(i * size, size), size)


def rows_loop(total, size, body):
    def step(i, carry):
        body(i, span(i, size))
        return carry

    lax.fori_loop(0, total // size, step, 0)


def forward_kernel(count, chunks, times, refs_in, refs_out, scratch, slopes):
    (qkv, proj, up, down, small, x, cot) = refs_in
    (qkv_o, proj_o, up_o, down_o, vec_o, cot_o, a1_o, q_o, k_o, v_o, o_o, lse_o, x2_o, a2_o, u_o, gp_o, gdown_o) = refs_out
    (qkv_w, proj_w, up_w, down_w, vec, vland, x_f, cot_f, a1, q, k, v, vt, ot, o, lse, part, part_r, x2, a2, u, gp, gdown, pos,
     send, recv, vsend, vrecv, psend, precv, own_sem, out_sem) = scratch
    me = lax.axis_index("dp")
    t = lax.axis_index("tensor")
    other = 1 - t
    mine = bits_of(me, count)
    orders = [order[::-1] for order in halving_orders(count)]
    full = block_index(mine, (), count)
    tokens, model = x_f.shape
    width = q.shape[1]
    hidden = u.shape[1]
    heads = width // HD
    local_rows = x.shape[0]
    mesh_copy = functools.partial(pltpu.make_async_remote_copy, device_id_type=MESH)

    enter(me, mine, count, other)
    waits = []

    def vec_step(s):
        to = {"dp": partner_of(me, mine, s)} if s < count else {"tensor": other}
        return mesh_copy(small if s == 0 else vec.at[s], vland.at[s], vsend.at[s], vrecv.at[s], device_id=to)

    vec[0] = small[...]
    vec_copies = [vec_step(s) for s in range(count + 1)]
    vec_copies[0].start()

    mine_rows = pl.ds(t * local_rows, local_rows)
    pair_copies = [mesh_copy(src, dst.at[mine_rows], psend.at[i], precv.at[i], device_id={"tensor": other})
                   for i, (src, dst) in enumerate(((x, x_f), (cot, cot_f)))]
    for copy in pair_copies:
        copy.start()

    names = {"qkv": (qkv, qkv_w), "proj": (proj, proj_w), "up": (up, up_w), "down": (down, down_w)}

    def views(c):
        name, lead, lo, size = chunks[c]
        src, dst = names[name]
        if lead is not None:
            src, dst = src.at[lead], dst.at[lead]
        return src.at[:, pl.ds(lo, size)], dst, (slice(None), pl.ds(lo, size))

    def copy_of(c, s):
        order = orders[GATHER_MODES[c % len(GATHER_MODES)]]
        src, dst, tail = views(c)
        at = (*block_index(mine, order[:s], count), *tail)
        return mesh_copy(src if s == 0 else dst.at[at], dst.at[at], send.at[c * count + s], recv.at[c * count + s],
                         device_id={"dp": partner_of(me, mine, order[s])})

    owns = [pltpu.make_async_copy(src, dst.at[full], own_sem.at[i]) for i, (src, dst) in enumerate(
        [(qkv.at[c], qkv_w.at[c]) for c in range(3)] + [(proj, proj_w), (up, up_w), (down, down_w)])]
    owns += [pltpu.make_async_copy(src, dst.at[mine_rows], own_sem.at[6 + i]) for i, (src, dst) in enumerate(((x, x_f), (cot, cot_f)))]
    for copy in owns:
        copy.start()
    for copy in owns:
        copy.wait()

    steps = sorted(((c, s) for c in range(len(chunks)) for s in range(count)), key=lambda cs: (cs[0] + GATHER_LOOK * cs[1], cs[0]))
    span_key = len(chunks) + GATHER_LOOK * count
    pace = lambda c, s: times["lead"] + (c + GATHER_LOOK * s) / span_key * times["gather"]
    queue = [(pace(c, s), c, s) for c, s in steps]
    done = set()
    clock = [0.0]

    def settle(c):
        if c not in done:
            while any(item[1] == c for item in queue):
                run(queue.pop(0))
            copy_of(c, count - 1).wait_recv()
            done.add(c)
            clock[0] = max(clock[0], pace(c, count))

    def run(item):
        at, c, s = item
        if s > 0:
            copy_of(c, s - 1).wait_recv()
        copy_of(c, s).start()

    def due(now):
        batch = []
        while queue and queue[0][0] <= now:
            batch.append(queue.pop(0))
        return batch

    def advance(cost):
        clock[0] += cost
        for item in due(clock[0]):
            run(item)

    outs = []

    def emit(src, dst):
        copy = pltpu.make_async_copy(src, dst, out_sem.at[len(outs)])
        copy.start()
        outs.append(copy)

    advance(times["lead"])
    for s in range(count):
        vec_copies[s].wait_recv()
        vec[s + 1] = vec[s] + vland[s]
        vec_copies[s + 1].start()
        advance(2.0)
    for copy in pair_copies:
        copy.wait_recv()
    emit(cot_f, cot_o)
    vec_copies[count].wait_recv()
    vec[count + 1, 0:8] = vec[count, 0:8] + vland[count, 0:8]
    vec[count + 1, 8:16] = vec[count, 8:16]
    emit(vec.at[count + 1], vec_o)
    table = vec.at[count + 1]

    def normed(rows_value, gain, shift):
        center = rows_value - jnp.mean(rows_value, axis=-1, keepdims=True)
        spread = jnp.mean(center * center, axis=-1, keepdims=True)
        return (center * lax.rsqrt(spread + epsilon)) * gain + shift

    def norm_one(i, rows):
        a1[rows, :] = normed(x_f[rows, :].astype(F32), table[0:1, :], table[2:3, :]).astype(BF)

    rows_loop(tokens, 256, norm_one)
    emit(a1, a1_o)
    pos[...] = lax.broadcasted_iota(jnp.int32, pos.shape, 0).astype(F32)
    advance(times["norm"])

    for c, dst in ((1, k), (0, q), (2, v)):
        for i, chunk in enumerate(chunks):
            if chunk[0] == "qkv" and chunk[1] == c:
                settle(i)

        def mix(i, rows, c=c, dst=dst):
            value = dot_nn(a1[rows, :], qkv_w[c].reshape(model, width))
            if c == 0:
                value = (value + table[10:11, 0:width]).astype(BF).astype(F32) * HD ** (-0.5)
            if c == 2:
                value = value + table[10:11, width : 2 * width]
            dst[rows, :] = value.astype(BF)
            if c == 2:
                vt[:, rows] = value.T.astype(BF)

        rows_loop(tokens, TILE, mix)
        advance(times["mix"])
    for src, dst in ((q, q_o), (k, k_o), (v, v_o), (qkv_w, qkv_o)):
        emit(src, dst)

    blocks = tokens // QB
    lane_half = lax.broadcasted_iota(jnp.int32, (QB, 2 * HD), 1) // HD
    batches = []
    for h in range(heads):
        batches.append(due(clock[0]))
        clock[0] += times["head"]

    def head_step(h, carry):
        for j in range(heads):
            if batches[j]:

                @pl.when(h == j)
                def _():
                    for item in batches[j]:
                        run(item)

        cols = span(h // 2, 2 * HD)
        slope = slopes[h]
        head_rows = span(h, HD)
        for b in range(blocks):
            end = (b + 1) * QB
            query = jnp.where(lane_half == lax.rem(h, 2), q[b * QB : end, cols], jnp.zeros((QB, 2 * HD), BF))
            bias = pos[0:end, :] * slope
            bias = jnp.concatenate([bias] * (QB // bias.shape[1]), axis=1)
            scores = dot_nt(k[0:end, cols], query) + bias
            diag = scores[b * QB : end, :]
            keep = lax.broadcasted_iota(jnp.int32, (QB, QB), 0) <= lax.broadcasted_iota(jnp.int32, (QB, QB), 1)
            diag = jnp.where(keep, diag, -1e30)
            scores = diag if b == 0 else jnp.concatenate([scores[0 : b * QB, :], diag], axis=0)
            peak = jnp.max(scores, axis=0, keepdims=True)
            weights = jnp.exp(scores - peak)
            total = jnp.sum(weights, axis=0, keepdims=True)
            out = dot_nn(vt[head_rows, 0:end], weights.astype(BF))
            ot[head_rows, b * QB : end] = (out / total).astype(BF)
            lse[pl.ds(h, 1), b * QB : end] = peak + jnp.log(total)
        return carry

    lax.fori_loop(0, heads, head_step, 0)
    for i, chunk in enumerate(chunks):
        if chunk[0] == "proj":
            settle(i)

    def turn(i, rows):
        o[rows, :] = ot[:, rows].astype(F32).T.astype(BF)

    rows_loop(tokens, TILE, turn)
    emit(o, o_o)
    emit(lse, lse_o)
    emit(proj_w, proj_o)

    def project(i, rows):
        part[rows, :] = dot_nt(o[rows, :], proj_w[...].reshape(model, width)).astype(BF)

    half = tokens // 2
    part_copies = []
    for j in range(2):
        project(j, pl.ds(j * half, half))
        copy = mesh_copy(part.at[pl.ds(j * half, half)], part_r.at[pl.ds(j * half, half)], psend.at[2 + j], precv.at[2 + j],
                         device_id={"tensor": other})
        copy.start()
        part_copies.append(copy)
    advance(times["proj"])
    for j in range(2):
        part_copies[j].wait_recv()

        def norm_two(i, rows, j=j):
            rows = pl.ds(pl.multiple_of(j * half + i * 256, 256), 256)
            middle = x_f[rows, :].astype(F32) + (part[rows, :].astype(F32) + part_r[rows, :].astype(F32)) + table[3:4, :]
            x2[rows, :] = middle
            a2[rows, :] = normed(middle, table[1:2, :], table[4:5, :]).astype(BF)

        rows_loop(half, 256, norm_two)
        advance(times["norm"])
    emit(x2, x2_o)
    emit(a2, a2_o)

    for j in range(hidden // TILE):
        cols = slice(j * TILE, (j + 1) * TILE)
        for i, chunk in enumerate(chunks):
            if chunk[0] == "up" and j * TILE <= chunk[2] < (j + 1) * TILE:
                settle(i)

        row = 8 + j * TILE // model
        bias_at = j * TILE % model

        def expand(i, rows, cols=cols, row=row, bias_at=bias_at):
            pre = dot_nn(a2[rows, :], up_w[..., cols].reshape(model, TILE)) + table[row : row + 1, bias_at : bias_at + TILE]
            square = pre * pre
            bent = jnp.tanh(pre * (gelu_scale + (gelu_scale * 0.044715) * square))
            rise = 0.5 + 0.5 * bent
            u[rows, cols] = (pre * rise).astype(BF)
            slope = 0.5 * pre * (1.0 - bent * bent) * (gelu_scale + (3 * 0.044715 * gelu_scale) * square)
            gp[rows, cols] = (rise + slope).astype(BF)

        rows_loop(tokens, 256, expand)
        advance(times["up"])

        def sum_down(i, rows, cols=cols):
            gdown[rows, cols] = dot_tn(cot_f[:, rows], u[:, cols]).astype(BF)

        rows_loop(model, TILE, sum_down)
        advance(times["down"])
    for src, dst in ((u, u_o), (gp, gp_o), (up_w, up_o), (gdown, gdown_o)):
        emit(src, dst)
    for i in range(len(chunks)):
        settle(i)
    emit(down_w, down_o)
    for c in range(len(chunks)):
        for s in range(count):
            copy_of(c, s).wait_send()
    for copy in vec_copies + pair_copies + part_copies:
        copy.wait_send()
    for copy in outs:
        copy.wait()


TIMES = {"gather": 115.0, "lead": 3.0, "mix": 1.5, "head": 2.0, "proj": 2.5, "norm": 2.5, "up": 3.0, "down": 1.5}


def forward_all(slopes, qkv, proj, up, down, small, x, cot, n, width=256, times=TIMES):
    count = n.bit_length() - 1
    two = (2,) * count
    chunks = []
    for c in (1, 0, 2):
        chunks += [("qkv", c, lo, width) for lo in range(0, qkv.shape[2], width)]
    for name, a in (("proj", proj), ("up", up), ("down", down)):
        chunks += [(name, None, lo, width) for lo in range(0, a.shape[1], width)]
    tokens, model = 2 * x.shape[0], x.shape[1]
    inner, hidden = qkv.shape[2], up.shape[1]
    heads = inner // HD
    weights = [((3, *two, *qkv.shape[1:]), BF), ((*two, *proj.shape), BF), ((*two, *up.shape), BF), ((*two, *down.shape), BF)]
    shapes = weights + [((16, model), F32), ((tokens, model), BF), ((tokens, model), BF)] + [((tokens, inner), BF)] * 4
    shapes += [((heads, tokens), F32), ((tokens, model), F32), ((tokens, model), BF), ((tokens, hidden), BF), ((tokens, hidden), BF), ((model, hidden), BF)]
    vm = lambda s, d: pltpu.VMEM(s, d)
    scratch = [vm(*w) for w in weights]
    scratch += [vm((count + 2, 16, model), F32), vm((count + 1, 16, model), F32), vm((tokens, model), BF), vm((tokens, model), BF), vm((tokens, model), BF)]
    scratch += [vm((tokens, inner), BF)] * 3 + [vm((inner, tokens), BF)] * 2 + [vm((tokens, inner), BF), vm((heads, tokens), F32)]
    scratch += [vm((tokens, model), BF)] * 2 + [vm((tokens, model), F32), vm((tokens, model), BF), vm((tokens, hidden), BF), vm((tokens, hidden), BF), vm((model, hidden), BF)]
    scratch += [vm((tokens, 128), F32)]
    sems = lambda k: pltpu.SemaphoreType.DMA((k,))
    k = len(chunks) * count
    scratch += [sems(k), sems(k), sems(count + 1), sems(count + 1), sems(4), sems(4), sems(8), sems(len(shapes))]

    def body(slopes_ref, *refs):
        forward_kernel(count, chunks, times, refs[:7], refs[7 : 7 + len(shapes)], refs[7 + len(shapes) :], slopes_ref)

    return pl.pallas_call(
        body, out_shape=tuple(jax.ShapeDtypeStruct(*s) for s in shapes),
        in_specs=[pl.BlockSpec(memory_space=pltpu.SMEM)] + [VM] * 7, out_specs=[ANY] * len(shapes), scratch_shapes=scratch,
        compiler_params=pltpu.CompilerParams(collective_id=0, has_side_effects=True, vmem_limit_bytes=62 * 2**20), name="forward_all",
    )(slopes, qkv, proj, up, down, small, x, cot)

SCATTER_MODES = (0, 1, 0, 1, 0, 1, 0, 2)


def backward_kernel(count, chunks, times, slopes, table, refs_in, refs_out, scratch):
    (x_h, cot_h, a1_h, q_h, k_h, v_h, o_h, lse_h, x2_h, a2_h, u_h, gp_h, gdown_h, qkv_h, proj_h, up_h, down_h) = refs_in
    (layer_o, grad_o, gqkv_o, gproj_o, gup_o, gdown_o, sums_o) = refs_out
    landing = scratch[:count]
    (sums, sland, x_f, cot, a1, lse, x2, gp, big, gdown, gproj, gqkv, wide, up_w, part, part_r, first_r, last_r,
     kt, dqt, acc_k, acc_v, pos, send, recv, vsend, vrecv, psend, precv, in_sem) = scratch[count:]
    me = lax.axis_index("dp")
    t = lax.axis_index("tensor")
    other = 1 - t
    mine = bits_of(me, count)
    orders = halving_orders(count)
    tokens, model = cot.shape
    width = q_h.shape[1]
    hidden = gp.shape[1]
    heads = width // HD
    local = tokens // 2
    q, k, v, o = (up_w.at[:, pl.ds(i * width, width)] for i in range(4))
    dq, dk, dv, do = q, k, v, o
    mesh_copy = functools.partial(pltpu.make_async_remote_copy, device_id_type=MESH)
    rows_of = lambda who, i, size: pl.ds(pl.multiple_of(who * local + i * size, size), size)

    enter(me, mine, count, other)
    loads = {}

    def load(name, src, dst):
        copy = pltpu.make_async_copy(src, dst, in_sem.at[len(loads)])
        copy.start()
        loads[name] = copy

    load("u", u_h, big)
    load("down", down_h, wide)
    load("gdown", gdown_h, gdown)
    load("cot", cot_h, cot)
    load("gp", gp_h, gp)
    load("x2", x2_h, x2)
    load("a2", a2_h, a1)
    load("up", up_h, up_w)
    load("lse", lse_h, lse)
    load("x", x_h, x_f)

    grads = {"qkv": gqkv, "proj": gproj, "up": big, "down": gdown}
    finals = {"qkv": gqkv_o, "proj": gproj_o, "up": gup_o, "down": gdown_o}
    size = chunks[0][3]

    def order_of(c):
        return orders[SCATTER_MODES[c % len(SCATTER_MODES)]]

    def held(c):
        name, lead, lo, _ = chunks[c]
        ref = grads[name]
        return ref if lead is None else ref.at[lead]

    def region(c, s, flip):
        order = order_of(c)
        at = []
        for b in reversed(range(count)):
            if b == order[s]:
                at.append(1 - mine[b] if flip else mine[b])
            else:
                at.append(mine[b] if b in order[:s] else slice(None))
        return tuple(at)

    def copy_of(c, s):
        name, lead, lo, _ = chunks[c]
        src = held(c)
        if name == "down" and s == 0:
            src = gdown_h
        at = (*region(c, s, True), slice(None), pl.ds(lo, size))
        return mesh_copy(src.at[at], landing[s].at[c], send.at[c * count + s], recv.at[c * count + s],
                         device_id={"dp": partner_of(me, mine, order_of(c)[s])})

    def run(item):
        at, c, s = item
        name, lead, lo, _ = chunks[c]
        copy_of(c, s - 1).wait_recv()
        got = landing[s - 1].at[c]
        keep = region(c, s - 1, False)
        cols = slice(lo, lo + size)
        ref = held(c)
        if s == count:
            total = ref[(*keep, slice(None), cols)].astype(F32) + got[...].astype(F32)
            out = finals[name]
            if lead is not None:
                out = out.at[lead]
            out[:, cols] = total
            return
        left = count - s

        def add(i, carry):
            sub = [lax.rem(i // (1 << (left - 1 - j)), 2) for j in range(left)]
            it = iter(sub)
            at = (*(next(it) if isinstance(b, slice) else b for b in keep), slice(None), cols)
            ref[at] = (ref[at].astype(F32) + got[tuple(sub)].astype(F32)).astype(BF)
            return carry

        lax.fori_loop(0, 1 << left, add, 0)
        copy_of(c, s).start()

    queue = []
    clock = [times["lead"]]
    slot = [0.0]
    each = times["scatter"] / len(chunks)

    def ready(names):
        for c, (name, lead, lo, _) in enumerate(chunks):
            if (name, lead, lo) in names:
                slot[0] = max(clock[0], slot[0] + each)
                copy_of(c, 0).start()
                queue.extend((slot[0] + s * times["step"], c, s) for s in range(1, count + 1))
        queue.sort()

    def due():
        batch = []
        while queue and queue[0][0] <= clock[0]:
            batch.append(queue.pop(0))
        return batch

    def advance(cost):
        clock[0] += cost
        for item in due():
            run(item)

    tiles = lambda name, total, lead=None, at=0: {(name, lead, lo) for lo in range(at, at + total, size)}
    ready(tiles("down", hidden))
    loads["gdown"].wait()
    sums[0] = jnp.zeros_like(sums[0])
    pos[...] = lax.broadcasted_iota(jnp.int32, pos.shape, 0).astype(F32)

    def whole(ref, h=None, cols=slice(None)):
        return ref[:, cols] if h is None else ref[h * (model // 2) : (h + 1) * (model // 2), cols]

    loads["u"].wait()
    loads["down"].wait()
    half = model // 2

    def lowered(who, h):
        return dot_nt(big[who].reshape(local, hidden), whole(wide, h))

    for h in range(2):
        part[0:local, h * half : (h + 1) * half] = lowered(other, h).astype(BF)
    first = mesh_copy(part.at[pl.ds(0, local)], first_r, psend.at[0], precv.at[0], device_id={"tensor": other})
    first.start()
    advance(times["half"])

    loads["cot"].wait()
    loads["gp"].wait()
    for j in range(hidden // TILE):
        cols = slice(j * TILE, (j + 1) * TILE)

        def grad_pre(i, rows, cols=cols):
            value = (dot_nn(cot[rows, :], whole(wide, cols=cols)) * gp[rows, cols].astype(F32)).astype(BF)
            gp[rows, cols] = value
            line = 8 + cols.start // model
            at = slice(cols.start % model, cols.start % model + TILE)
            sums[0, line : line + 1, at] += jnp.sum(value.astype(F32), axis=0, keepdims=True)

        rows_loop(tokens, 256, grad_pre)
        advance(times["quarter"])

    loads["x2"].wait()
    first.wait_recv()
    for h in range(2):
        cols = slice(h * half, (h + 1) * half)
        mid = x2[rows_of(t, 0, local), cols]
        layer_o[:, cols] = (mid + (lowered(t, h) + first_r[:, cols].astype(F32)) + table[5:6, cols]).astype(BF)
    advance(times["half"])
    load("qkv", qkv_h.at[0], wide.at[:, pl.ds(0, width)])
    load("qkv1", qkv_h.at[1], wide.at[:, pl.ds(width, width)])
    load("qkv2", qkv_h.at[2], wide.at[:, pl.ds(2 * width, width)])
    load("proj", proj_h, wide.at[:, pl.ds(3 * width, width)])

    loads["a2"].wait()
    loads["up"].wait()
    first.wait_send()
    part_copies = []
    for h in range(2):
        rows = pl.ds(h * local, local)
        for e in range(2):
            part[rows, e * half : (e + 1) * half] = dot_nt(gp[rows, :], whole(up_w, e)).astype(BF)
        copy = mesh_copy(part.at[rows], part_r.at[rows], psend.at[1 + h], precv.at[1 + h], device_id={"tensor": other})
        copy.start()
        part_copies.append(copy)
        advance(times["half"])
    for name, src, dst in (("q", q_h, q), ("k", k_h, k), ("v", v_h, v), ("o", o_h, o)):
        load(name, src, dst)
    for j in range(hidden // TILE):
        cols = slice(j * TILE, (j + 1) * TILE)
        for h in range(2):
            value = dot_tn(a1[:, h * half : (h + 1) * half], gp[:, cols]).astype(BF)
            big[(h, Ellipsis, cols)] = value.reshape(*big.shape[1:-1], TILE)
        ready(tiles("up", TILE, at=j * TILE))
        advance(times["quarter"])
    load("a1", a1_h, a1)

    def norm_parts(value):
        center = value - jnp.mean(value, axis=-1, keepdims=True)
        inverse = lax.rsqrt(jnp.mean(center * center, axis=-1, keepdims=True) + epsilon)
        return center * inverse, inverse

    def norm_back(grad, normed, inverse, gain):
        scaled = grad * gain
        return inverse * (scaled - jnp.mean(scaled, axis=-1, keepdims=True) - normed * jnp.mean(scaled * normed, axis=-1, keepdims=True))

    def add_sum(line, value):
        sums[0, line : line + 1, :] += jnp.sum(value, axis=0, keepdims=True)

    for copy in part_copies:
        copy.wait_recv()
    for who, count_it in ((t, True), (other, False)):

        def through(i, carry, who=who, count_it=count_it):
            rows = rows_of(who, i, 128)
            grad = part[rows, :].astype(F32) + part_r[rows, :].astype(F32)
            normed, inverse = norm_parts(x2[rows, :])
            outer = cot[rows, :].astype(F32)
            mid = outer + norm_back(grad, normed, inverse, table[1:2, :])
            x2[rows, :] = mid
            cot[rows, :] = mid.astype(BF)
            if count_it:
                add_sum(1, grad * normed)
                add_sum(3, mid)
                add_sum(4, grad)
                add_sum(5, outer)
            return carry

        lax.fori_loop(0, local // 128, through, 0)
        advance(times["norm"])
    gx2 = cot

    loads["proj"].wait()
    loads["o"].wait()
    proj_cols = slice(3 * width, 4 * width)
    for h in range(2):
        gproj[h] = dot_tn(gx2[:, h * half : (h + 1) * half], o[...]).astype(BF).reshape(gproj.shape[1:])
    ready(tiles("proj", width))
    advance(times["small"])

    def through_proj(i, rows):
        do[rows, :] = dot_nn(gx2[rows, :], whole(wide, cols=proj_cols)).astype(BF)

    rows_loop(tokens, TILE, through_proj)
    for name in ("q", "k", "v", "lse"):
        loads[name].wait()

    def turn_keys(i, rows):
        kt[:, rows] = k[rows, :].astype(F32).T.astype(BF)

    rows_loop(tokens, TILE, turn_keys)
    advance(times["small"])

    blocks = tokens // QB
    lane_half = lax.broadcasted_iota(jnp.int32, (QB, 2 * HD), 1) // HD
    batches = []
    for h in range(heads):
        batches.append(due())
        clock[0] += times["head"]

    def head_step(h, carry):
        for j in range(heads):
            if batches[j]:

                @pl.when(h == j)
                def _():
                    for item in batches[j]:
                        run(item)

        cols = span(h // 2, 2 * HD)
        head_rows = span(h, HD)
        side = lax.rem(h, 2)
        slope = slopes[h]

        @pl.when(side == 0)
        def _():
            acc_k[...] = jnp.zeros_like(acc_k)
            acc_v[...] = jnp.zeros_like(acc_v)

        for b in range(blocks):
            end = (b + 1) * QB
            rows = slice(b * QB, end)
            zero = jnp.zeros((QB, 2 * HD), BF)
            query = jnp.where(lane_half == side, q[rows, cols], zero)
            outer = jnp.where(lane_half == side, do[rows, cols], zero)
            bias = pos[0:end, :] * slope
            bias = jnp.concatenate([bias] * (QB // bias.shape[1]), axis=1)
            scores = dot_nt(k[0:end, cols], query) + bias - lse[pl.ds(h, 1), rows]
            keep = lax.broadcasted_iota(jnp.int32, (QB, QB), 0) <= lax.broadcasted_iota(jnp.int32, (QB, QB), 1)
            diag = jnp.where(keep, scores[b * QB : end, :], -1e30)
            scores = diag if b == 0 else jnp.concatenate([scores[0 : b * QB, :], diag], axis=0)
            probs = jnp.exp(scores)
            acc_v[0:end, :] += dot_nn(probs.astype(BF), outer)
            grad = dot_nt(v[0:end, cols], outer)
            inner = jnp.sum(probs * grad, axis=0, keepdims=True)
            low = (probs * (grad - inner)).astype(BF)
            acc_k[0:end, :] += dot_nn(low, query)
            dqt[head_rows, rows] = (dot_nn(kt[head_rows, 0:end], low) * HD ** (-0.5)).astype(BF)

        @pl.when(side == 1)
        def _():
            dk[:, cols] = acc_k[...].astype(BF)
            dv[:, cols] = acc_v[...].astype(BF)

        return carry

    lax.fori_loop(0, heads, head_step, 0)

    def turn(i, rows):
        dq[rows, :] = dqt[:, rows].astype(F32).T.astype(BF)

    rows_loop(tokens, TILE, turn)
    loads["a1"].wait()
    for c, ref in ((1, dk), (2, dv), (0, dq)):
        for h in range(2):
            gqkv[c, h] = dot_tn(a1[:, h * half : (h + 1) * half], ref[...]).astype(BF).reshape(gqkv.shape[2:])
        ready(tiles("qkv", width, lead=c))
        advance(times["small"])
    for at, ref in ((0, dq), (width, dv)):
        sums[0, 10:11, at : at + width] = jnp.sum(ref[...].astype(F32), axis=0, keepdims=True)

    for name in ("qkv", "qkv1", "qkv2"):
        loads[name].wait()

    def back_one(rows):
        total = dot_nt(dq[rows, :], whole(wide, cols=slice(0, width)))
        total += dot_nt(dk[rows, :], whole(wide, cols=slice(width, 2 * width)))
        return total + dot_nt(dv[rows, :], whole(wide, cols=slice(2 * width, 3 * width)))

    for copy in part_copies:
        copy.wait_send()

    def partner_rows(i, carry):
        part[span(i, 256), :] = back_one(rows_of(other, i, 256)).astype(BF)
        return carry

    lax.fori_loop(0, local // 256, partner_rows, 0)
    last = mesh_copy(part.at[pl.ds(0, local)], last_r, psend.at[3], precv.at[3], device_id={"tensor": other})
    last.start()
    advance(times["half"])
    loads["x"].wait()
    last.wait_recv()

    def own_rows(i, carry):
        rows = rows_of(t, i, 256)
        here = span(i, 256)
        grad = back_one(rows) + last_r[here, :].astype(F32)
        normed, inverse = norm_parts(x_f[here, :].astype(F32))
        grad_o[here, :] = x2[rows, :] + norm_back(grad, normed, inverse, table[0:1, :])
        add_sum(0, grad * normed)
        add_sum(2, grad)
        return carry

    lax.fori_loop(0, local // 256, own_rows, 0)
    advance(times["half"])

    def sum_step(s):
        to = {"dp": partner_of(me, mine, s)} if s < count else {"tensor": other}
        return mesh_copy(sums.at[s], sland.at[s], vsend.at[s], vrecv.at[s], device_id=to)

    sum_copies = [sum_step(s) for s in range(count + 1)]
    sum_copies[0].start()
    for s in range(count):
        advance(times["hop"])
        sum_copies[s].wait_recv()
        sums[s + 1] = sums[s] + sland[s]
        sum_copies[s + 1].start()
    while queue:
        run(queue.pop(0))
    sum_copies[count].wait_recv()
    sums_o[0:8, :] = sums[count, 0:8] + sland[count, 0:8]
    sums_o[8:16, :] = sums[count, 8:16]
    for c in range(len(chunks)):
        for s in range(count):
            copy_of(c, s).wait_send()
    for copy in sum_copies + [last]:
        copy.wait_send()


BACK_TIMES = {"scatter": 110.0, "step": 13.0, "lead": 3.0, "half": 3.0, "quarter": 1.7, "norm": 2.5, "small": 2.0, "head": 4.0, "hop": 2.5}


def backward_all(slopes, table, x, cot, a1, q, k, v, o, lse, x2, a2, u, gp, gdown, qkv_w, proj_w, up_w, down_w, n, width=256, times=BACK_TIMES):
    count = n.bit_length() - 1
    two = (2,) * count
    tokens, model = cot.shape
    inner, hidden = q.shape[1], gp.shape[1]
    heads = inner // HD
    r = model // n
    chunks = [("down", None, lo, width) for lo in range(0, hidden, width)]
    chunks += [("up", None, lo, width) for lo in range(0, hidden, width)]
    chunks += [("proj", None, lo, width) for lo in range(0, inner, width)]
    for c in (1, 2, 0):
        chunks += [("qkv", c, lo, width) for lo in range(0, inner, width)]
    f = lambda *s: jax.ShapeDtypeStruct(s, F32)
    outs = (jax.ShapeDtypeStruct(x.shape, BF), f(*x.shape), f(3, r, inner), f(r, inner), f(r, hidden), f(r, hidden), f(16, model))
    vm = lambda *s, d=BF: pltpu.VMEM(s, d)
    scratch = [vm(len(chunks), *two[: count - 1 - s], r, width) for s in range(count)]
    scratch += [vm(count + 1, 16, model, d=F32), vm(count + 1, 16, model, d=F32), vm(*x.shape), vm(tokens, model), vm(tokens, model)]
    scratch += [vm(heads, tokens, d=F32), vm(tokens, model, d=F32), vm(tokens, hidden)]
    scratch += [vm(*two, r, hidden), vm(*two, r, hidden), vm(*two, r, inner), vm(3, *two, r, inner), vm(model, hidden), vm(model, hidden)]
    scratch += [vm(tokens, model), vm(tokens, model), vm(*x.shape), vm(*x.shape), vm(inner, tokens), vm(inner, tokens)]
    scratch += [vm(tokens, 2 * HD, d=F32)] * 2 + [vm(tokens, 128, d=F32)]
    sems = lambda m: pltpu.SemaphoreType.DMA((m,))
    m = len(chunks) * count
    scratch += [sems(m), sems(m), sems(count + 1), sems(count + 1), sems(4), sems(4), sems(20)]
    flat = lambda a: a.reshape(*a.shape[: a.ndim - count - 2], model, a.shape[-1])
    by_block = lambda a: a.reshape(*two, r, a.shape[-1])

    def body(slopes_ref, table_ref, *refs):
        backward_kernel(count, chunks, times, slopes_ref, table_ref, refs[:17], refs[17 : 17 + len(outs)], refs[17 + len(outs) :])

    return pl.pallas_call(
        body, out_shape=outs, in_specs=[pl.BlockSpec(memory_space=pltpu.SMEM), VM] + [ANY] * 17, out_specs=[VM] * len(outs), scratch_shapes=scratch,
        compiler_params=pltpu.CompilerParams(collective_id=1, has_side_effects=True, vmem_limit_bytes=67043328), name="backward_all",
    )(slopes, table, x, cot, a1, q, k, v, o, lse, x2, a2, by_block(u), gp, by_block(gdown), flat(qkv_w), flat(proj_w), flat(up_w), flat(down_w))

def on_device(layer_in, w_qkv, b_qv, w_proj, w_ff1, b_ff1, w_ff2, norm_gains, add_biases, cotangent):
    n = lax.axis_size("dp")
    i = lax.axis_index("dp")
    t = lax.axis_index("tensor")
    width = w_qkv.shape[2]
    model = layer_in.shape[1]
    hidden = w_ff1.shape[1]
    heads = b_qv.shape[1]
    part = norm_gains.shape[1]
    zero = jnp.int32(0)
    put = lambda shape, a, at: lax.dynamic_update_slice(jnp.zeros(shape, F32), a.astype(F32), at)
    up_grid = (b_ff1.shape[0], n * b_ff1.shape[1])
    qv_grid = (*b_qv.shape[:2], n * b_qv.shape[2])
    small = jnp.concatenate([
        put((8, model), jnp.concatenate([norm_gains, add_biases]), (zero, (2 * i + t) * part)),
        put(up_grid, b_ff1, (zero, i * b_ff1.shape[1])).reshape(-1, model),
        put(qv_grid, b_qv, (zero, zero, i * b_qv.shape[2])).reshape(-1, model),
        jnp.zeros((8 - (hidden + 2 * width) // model, model), F32)])
    slopes = 2.0 ** (-8.0 * (t * heads + jnp.arange(heads, dtype=jnp.int32) + 1).astype(F32) / H)
    (qkv_w, proj_w, up_w, down_w, vectors, cot, a1, q, k, v, o, lse, x2, a2, u, rise, grad_down) = forward_all(
        slopes, w_qkv, w_proj.T, w_ff1, w_ff2.T, small, layer_in, cotangent, n)
    layer_out, grad_in, out_qkv, out_proj, out_up, out_down, sums = backward_all(
        slopes, vectors, layer_in, cot, a1, q, k, v, o, lse, x2, a2, u, rise, grad_down, qkv_w, proj_w, up_w, down_w, n)
    own = lax.dynamic_slice(sums, (zero, (2 * i + t) * part), (6, part))
    up_sums = lax.dynamic_slice_in_dim(sums[8 : 8 + hidden // model].reshape(up_grid), i * b_ff1.shape[1], b_ff1.shape[1], 1)
    qv_sums = lax.dynamic_slice_in_dim(sums[10].reshape(qv_grid), i * b_qv.shape[2], b_qv.shape[2], 2)
    return (layer_out, grad_in, out_qkv, qv_sums, out_proj.T, out_up, up_sums, out_down.T, own[:2], own[2:])


def solution(mesh):
    rows, cols = P(("dp", "tensor"), None), P(None, ("dp", "tensor"))
    return jax.shard_map(
        on_device,
        mesh=mesh,
        in_specs=(rows, P(None, "dp", "tensor"), P(None, "tensor", "dp"), P("tensor", "dp"), P("dp", "tensor"),
                  P("tensor", "dp"), P("tensor", "dp"), cols, cols, rows),
        out_specs=(rows, rows, P(None, "dp", "tensor"), P(None, "tensor", "dp"), P("tensor", "dp"), P("dp", "tensor"),
                   P("tensor", "dp"), P("tensor", "dp"), cols, cols),
        check_vma=False,
    )
```

profile of v0, /device:TPU:0, one launch (start us, length us, event | category | flops | bytes accessed | tf_op | source)
XLA Modules:
  0.0 298.3 jit_solution(10275464357224932818)
XLA Ops:
  0.6 0.5 multiply_power_fusion.slopes_ref
  1.3 0.7 pad_maximum_fusion
  2.0 0.8 copy.21
  2.7 0.1 dynamic_update_slice.11
  2.9 0.8 copy.20
  3.7 0.2 dynamic_update_slice.10
  4.0 0.4 dynamic_update_slice.9
  4.5 0.7 maximum_maximum_fusion.refs_4_
  5.2 134.0 %forward_all.1 = (bf16[3,2,2,2,2,64,512]{6,5,4,3,2,1,0:T(8,128)(2,1)}, bf16[2,2,2,2,64,512]{5,4,3,2,1,0:T(8,128)(2,1)}, bf16[2,2,2,2,64,2048]{5,4,3,2,1,0:T(8,12...) custom-call(f32[8]{0:T(128)} %multiply_power_fusion.slopes_ref, ...), custom_call_target="tpu_custom_call" | custom-call | tf_op jit(solution)/shard_map/forward_all/pallas_call | solution.py:367
  139.2 145.3 %backward_all.1 = (bf16[512,1024]{1,0:T(8,128)(2,1)}, f32[512,1024]{1,0:T(8,128)}, f32[3,64,512]{2,1,0:T(8,128)}, f32[64,512]{1,0:T(8,128)}, f32[64,2048]{1,0:T(...) custom-call(f32[8]{0:T(128)} %multiply_power_fusion.slopes_ref, f32[16,1024]{1,0:T(8,128)} %get-tuple-element.34.table_ref, ...), custom_call_target="tpu_custom_call" | custom-call | tf_op jit(solution)/shard_map/backward_all/pallas_call | solution.py:785
  284.5 0.8 constant_dynamic-slice_fusion
  285.3 0.6 slice.14
  285.9 0.6 slice.15
  286.5 0.8 slice_reduce_fusion
  287.2 0.8 slice.13
  288.2 0.7 copy.24
  288.8 0.1 reshape.55
  289.0 0.7 copy.25
  289.6 2.3 copy.35
  292.0 3.2 %copy.36 = f32[512,1024]{1,0:T(8,128)} copy(f32[512,1024]{1,0:T(8,128)} %get-tuple-element.69) | data formatting | bytes 4194304
  295.1 0.7 copy.37
  295.9 0.7 copy.38
  296.5 0.8 copy.39
  297.3 0.8 copy.40
  (18 shorter events, 0.5 us)
Async XLA Ops:
  284.5 10.7 %copy-start.2 = (f32[3,64,512]{2,1,0:T(8,128)S(1)}, f32[3,64,512]{2,1,0:T(8,128)}, u32[]{:S(2)}) copy-start(f32[3,64,512]{2,1,0:T(8,128)} %get-tuple-element.70) | copy-start | bytes 1179652
  284.5 11.4 %copy-start.3 = (f32[64,512]{1,0:T(8,128)S(1)}, f32[64,512]{1,0:T(8,128)}, u32[]{:S(2)}) copy-start(f32[64,512]{1,0:T(8,128)} %get-tuple-element.55) | copy-start | bytes 393220
  284.5 12.1 %copy-start.1 = (f32[64,2048]{1,0:T(8,128)S(1)}, f32[64,2048]{1,0:T(8,128)}, u32[]{:S(2)}) copy-start(f32[64,2048]{1,0:T(8,128)} %get-tuple-element.73) | copy-start | bytes 1572868
  289.6 7.7 %copy-start = (f32[64,2048]{1,0:T(8,128)S(1)}, f32[64,2048]{1,0:T(8,128)}, u32[]{:S(2)}) copy-start(f32[64,2048]{1,0:T(8,128)} %get-tuple-element.57) | copy-start | bytes 1572868
where the time goes:
time: 304 us; the launch traced here: 298 us
  Pallas kernels  279 us (92%)
  local copies, waits for them, and re-layouts  16.2 us (5%)
    pallas_call x1, Pallas kernels, backward_all(): pl.pallas_call(body, out_shape=outs, in_specs=[pl.BlockSpec(memory_space=...  145 us
    pallas_call x1, Pallas kernels, forward_all(): pl.pallas_call(body, out_shape=tuple((jax.ShapeDtypeStruct(*s) for s in s...  134 us
    unnamed x16, local copies, waits for them, and re-layouts  9.81 us

commit v1 on v0

--- a/solution.py
+++ b/solution.py
@@ -44,8 +44,14 @@
 BF = jnp.bfloat16
 TILE = 512
 QB = 256
-GATHER_MODES = (0, 1, 0, 1, 0, 1, 0, 2)
-GATHER_LOOK = 4
+LOOK = 4
+
+
+def bit_orders(count, modes, total, flip):
+    if modes and count == 4:
+        return [[mode // 10**i % 10 for i in (3, 2, 1, 0)] for mode in modes]
+    cyclic = [[(start + i) % count for i in range(count)] for start in (0, 1, 0, 1, 0, 1, 0, 2)]
+    return [(order[::-1] if flip else order) for order in (cyclic[c % len(cyclic)] for c in range(total))]
 
 
 def dot_nn(a, b):
@@ -62,6 +68,22 @@
 
 def span(i, size):
     return pl.ds(pl.multiple_of(i * size, size), size)
+
+
+def paced_loop(steps, body, batches, run):
+    def step(i, carry):
+        for j in range(steps):
+            if batches[j]:
+
+                @pl.when(i == j)
+                def _():
+                    for item in batches[j]:
+                        run(item)
+
+        body(i)
+        return carry
+
+    lax.fori_loop(0, steps, step, 0)
 
 
 def rows_loop(total, size, body):
@@ -72,7 +94,7 @@
     lax.fori_loop(0, total // size, step, 0)
 
 
-def forward_kernel(count, chunks, times, refs_in, refs_out, scratch, slopes):
+def forward_kernel(count, chunks, modes, order, plan, refs_in, refs_out, scratch, slopes):
     (qkv, proj, up, down, small, x, cot) = refs_in
     (qkv_o, proj_o, up_o, down_o, vec_o, cot_o, a1_o, q_o, k_o, v_o, o_o, lse_o, x2_o, a2_o, u_o, gp_o, gdown_o) = refs_out
     (qkv_w, proj_w, up_w, down_w, vec, vland, x_f, cot_f, a1, q, k, v, vt, ot, o, lse, part, part_r, x2, a2, u, gp, gdown, pos,
@@ -81,7 +103,7 @@
     t = lax.axis_index("tensor")
     other = 1 - t
     mine = bits_of(me, count)
-    orders = [order[::-1] for order in halving_orders(count)]
+    orders = bit_orders(count, modes, len(chunks), True)
     full = block_index(mine, (), count)
     tokens, model = x_f.shape
     width = q.shape[1]
@@ -117,7 +139,7 @@
         return src.at[:, pl.ds(lo, size)], dst, (slice(None), pl.ds(lo, size))
 
     def copy_of(c, s):
-        order = orders[GATHER_MODES[c % len(GATHER_MODES)]]
+        order = orders[c]
         src, dst, tail = views(c)
         at = (*block_index(mine, order[:s], count), *tail)
         return mesh_copy(src if s == 0 else dst.at[at], dst.at[at], send.at[c * count + s], recv.at[c * count + s],
@@ -131,37 +153,35 @@
     for copy in owns:
         copy.wait()
 
-    steps = sorted(((c, s) for c in range(len(chunks)) for s in range(count)), key=lambda cs: (cs[0] + GATHER_LOOK * cs[1], cs[0]))
-    span_key = len(chunks) + GATHER_LOOK * count
-    pace = lambda c, s: times["lead"] + (c + GATHER_LOOK * s) / span_key * times["gather"]
-    queue = [(pace(c, s), c, s) for c, s in steps]
+    queue = [divmod(code, count) for code in order] if order and count == 4 else sorted(
+        ((c, s) for c in range(len(chunks)) for s in range(count)), key=lambda cs: (cs[0] + LOOK * cs[1], cs[0]))
+    share = list(plan) if plan and count == 4 else []
     done = set()
-    clock = [0.0]
+
+    def run(item):
+        c, s = item
+        if s > 0:
+            copy_of(c, s - 1).wait_recv()
+        copy_of(c, s).start()
 
     def settle(c):
         if c not in done:
-            while any(item[1] == c for item in queue):
+            while any(item[0] == c for item in queue):
                 run(queue.pop(0))
             copy_of(c, count - 1).wait_recv()
             done.add(c)
-            clock[0] = max(clock[0], pace(c, count))
-
-    def run(item):
-        at, c, s = item
-        if s > 0:
-            copy_of(c, s - 1).wait_recv()
-        copy_of(c, s).start()
-
-    def due(now):
-        batch = []
-        while queue and queue[0][0] <= now:
-            batch.append(queue.pop(0))
+
+    def due():
+        size = share.pop(0) if share else 2
+        batch, queue[:] = queue[:size], queue[size:]
         return batch
 
-    def advance(cost):
-        clock[0] += cost
-        for item in due(clock[0]):
+    def advance():
+        for item in due():
             run(item)
+
+    def paced(steps, body):
+        paced_loop(steps, body, [due() for _ in range(steps)], run)
 
     outs = []
 
@@ -170,12 +190,12 @@
         copy.start()
         outs.append(copy)
 
-    advance(times["lead"])
+    advance()
     for s in range(count):
         vec_copies[s].wait_recv()
         vec[s + 1] = vec[s] + vland[s]
         vec_copies[s + 1].start()
-        advance(2.0)
+        advance()
     for copy in pair_copies:
         copy.wait_recv()
     emit(cot_f, cot_o)
@@ -193,10 +213,9 @@
     def norm_one(i, rows):
         a1[rows, :] = normed(x_f[rows, :].astype(F32), table[0:1, :], table[2:3, :]).astype(BF)
 
-    rows_loop(tokens, 256, norm_one)
+    pos[...] = lax.broadcasted_iota(jnp.int32, pos.shape, 0).astype(F32)
+    paced(4, lambda i: norm_one(i, span(i, tokens // 4)))
     emit(a1, a1_o)
-    pos[...] = lax.broadcasted_iota(jnp.int32, pos.shape, 0).astype(F32)
-    advance(times["norm"])
 
     for c, dst in ((1, k), (0, q), (2, v)):
         for i, chunk in enumerate(chunks):
@@ -213,27 +232,14 @@
             if c == 2:
                 vt[:, rows] = value.T.astype(BF)
 
-        rows_loop(tokens, TILE, mix)
-        advance(times["mix"])
+        paced(2, lambda i: mix(i, span(i, tokens // 2)))
     for src, dst in ((q, q_o), (k, k_o), (v, v_o), (qkv_w, qkv_o)):
         emit(src, dst)
 
     blocks = tokens // QB
     lane_half = lax.broadcasted_iota(jnp.int32, (QB, 2 * HD), 1) // HD
-    batches = []
-    for h in range(heads):
-        batches.append(due(clock[0]))
-        clock[0] += times["head"]
-
-    def head_step(h, carry):
-        for j in range(heads):
-            if batches[j]:
-
-                @pl.when(h == j)
-                def _():
-                    for item in batches[j]:
-                        run(item)
-
+
+    def head_step(h):
         cols = span(h // 2, 2 * HD)
         slope = slopes[h]
         head_rows = span(h, HD)
@@ -253,9 +259,8 @@
             out = dot_nn(vt[head_rows, 0:end], weights.astype(BF))
             ot[head_rows, b * QB : end] = (out / total).astype(BF)
             lse[pl.ds(h, 1), b * QB : end] = peak + jnp.log(total)
-        return carry
-
-    lax.fori_loop(0, heads, head_step, 0)
+
+    paced(heads, head_step)
     for i, chunk in enumerate(chunks):
         if chunk[0] == "proj":
             settle(i)
@@ -279,23 +284,22 @@
                          device_id={"tensor": other})
         copy.start()
         part_copies.append(copy)
-    advance(times["proj"])
+        advance()
     for j in range(2):
         part_copies[j].wait_recv()
 
-        def norm_two(i, rows, j=j):
+        def norm_two(i, j=j):
             rows = pl.ds(pl.multiple_of(j * half + i * 256, 256), 256)
             middle = x_f[rows, :].astype(F32) + (part[rows, :].astype(F32) + part_r[rows, :].astype(F32)) + table[3:4, :]
             x2[rows, :] = middle
             a2[rows, :] = normed(middle, table[1:2, :], table[4:5, :]).astype(BF)
 
-        rows_loop(half, 256, norm_two)
-        advance(times["norm"])
+        paced(half // 256, norm_two)
     emit(x2, x2_o)
     emit(a2, a2_o)
 
     for j in range(hidden // TILE):
-        cols = slice(j * TILE, (j + 1) * TILE)
+        cols = pl.ds(j * TILE, TILE)
         for i, chunk in enumerate(chunks):
             if chunk[0] == "up" and j * TILE <= chunk[2] < (j + 1) * TILE:
                 settle(i)
@@ -312,19 +316,19 @@
             slope = 0.5 * pre * (1.0 - bent * bent) * (gelu_scale + (3 * 0.044715 * gelu_scale) * square)
             gp[rows, cols] = (rise + slope).astype(BF)
 
-        rows_loop(tokens, 256, expand)
-        advance(times["up"])
+        paced(tokens // 256, lambda i: expand(i, span(i, 256)))
 
         def sum_down(i, rows, cols=cols):
             gdown[rows, cols] = dot_tn(cot_f[:, rows], u[:, cols]).astype(BF)
 
-        rows_loop(model, TILE, sum_down)
-        advance(times["down"])
-    for src, dst in ((u, u_o), (gp, gp_o), (up_w, up_o), (gdown, gdown_o)):
-        emit(src, dst)
-    for i in range(len(chunks)):
+        paced(model // TILE, lambda i: sum_down(i, span(i, TILE)))
+        for src, dst in ((u, u_o), (gp, gp_o), (gdown, gdown_o)):
+            emit(src.at[:, cols], dst.at[:, cols])
+        emit(up_w.at[(Ellipsis, cols)], up_o.at[(Ellipsis, cols)])
+    for i, (name, lead, lo, size) in enumerate(chunks):
         settle(i)
-    emit(down_w, down_o)
+        if name == "down":
+            emit(down_w.at[(Ellipsis, pl.ds(lo, size))], down_o.at[(Ellipsis, pl.ds(lo, size))])
     for c in range(len(chunks)):
         for s in range(count):
             copy_of(c, s).wait_send()
@@ -334,10 +338,22 @@
         copy.wait()
 
 
-TIMES = {"gather": 115.0, "lead": 3.0, "mix": 1.5, "head": 2.0, "proj": 2.5, "norm": 2.5, "up": 3.0, "down": 1.5}
-
-
-def forward_all(slopes, qkv, proj, up, down, small, x, cot, n, width=256, times=TIMES):
+GATHER_MODES = (
+    3201, 1320, 3210, 2130, 2301, 3201, 3021, 1320, 3021, 3201, 3021, 1230, 2310, 3012, 3201, 1230, 3120, 2031, 1032, 2031, 321, 1230,
+    3210, 213,
+)
+GATHER_ORDER = (
+    16, 8, 20, 68, 17, 12, 9, 69, 40, 4, 21, 13, 0, 5, 70, 10, 18, 48, 36, 41, 14, 22, 84, 1, 28, 11, 19, 24, 6, 85, 42, 29, 49, 23,
+    32, 71, 44, 2, 37, 52, 64, 60, 7, 3, 86, 15, 25, 43, 30, 56, 76, 45, 88, 61, 38, 50, 92, 33, 53, 72, 65, 26, 31, 80, 39, 77, 93,
+    46, 87, 34, 57, 54, 62, 89, 51, 73, 27, 66, 94, 81, 78, 47, 35, 58, 55, 63, 90, 67, 74, 82, 95, 79, 59, 91, 75, 83,
+)
+GATHER_PLAN = (
+    41, 2, 3, 2, 2, 7, 0, 1, 0, 4, 0, 0, 1, 2, 2, 0, 4, 3, 3, 2, 1, 2, 1, 5, 0, 3, 1, 0, 0, 0, 0, 0, 1, 0, 1, 0, 0, 0, 1, 0, 0, 1, 0,
+    0, 0, 0, 0, 0, 0, 0, 0, 0, 0,
+)
+
+
+def forward_all(slopes, qkv, proj, up, down, small, x, cot, n, width=256):
     count = n.bit_length() - 1
     two = (2,) * count
     chunks = []
@@ -359,10 +375,10 @@
     scratch += [vm((tokens, 128), F32)]
     sems = lambda k: pltpu.SemaphoreType.DMA((k,))
     k = len(chunks) * count
-    scratch += [sems(k), sems(k), sems(count + 1), sems(count + 1), sems(4), sems(4), sems(8), sems(len(shapes))]
+    scratch += [sems(k), sems(k), sems(count + 1), sems(count + 1), sems(4), sems(4), sems(8), sems(64)]
 
     def body(slopes_ref, *refs):
-        forward_kernel(count, chunks, times, refs[:7], refs[7 : 7 + len(shapes)], refs[7 + len(shapes) :], slopes_ref)
+        forward_kernel(count, chunks, GATHER_MODES, GATHER_ORDER, GATHER_PLAN, refs[:7], refs[7 : 7 + len(shapes)], refs[7 + len(shapes) :], slopes_ref)
 
     return pl.pallas_call(
         body, out_shape=tuple(jax.ShapeDtypeStruct(*s) for s in shapes),
@@ -370,10 +386,23 @@
         compiler_params=pltpu.CompilerParams(collective_id=0, has_side_effects=True, vmem_limit_bytes=62 * 2**20), name="forward_all",
     )(slopes, qkv, proj, up, down, small, x, cot)
 
-SCATTER_MODES = (0, 1, 0, 1, 0, 1, 0, 2)
-
-
-def backward_kernel(count, chunks, times, slopes, table, refs_in, refs_out, scratch):
+SCATTER_MODES = (
+    123, 3012, 321, 213, 2310, 1203, 321, 1230, 2031, 1023, 132, 1032, 321, 1302, 1230, 231, 3102, 1023, 1032, 2013, 1032, 123, 1023,
+    213,
+)
+SCATTER_ORDER = (
+    1, 26, 11, 36, 2, 21, 27, 12, 37, 3, 46, 28, 6, 22, 41, 51, 56, 13, 31, 61, 16, 38, 4, 76, 7, 29, 71, 17, 47, 42, 23, 86, 57, 32,
+    39, 87, 77, 72, 52, 14, 62, 24, 33, 106, 48, 81, 91, 43, 8, 58, 96, 101, 66, 18, 116, 34, 111, 92, 73, 53, 78, 88, 97, 63, 102,
+    107, 9, 82, 112, 44, 59, 98, 74, 49, 79, 117, 64, 67, 93, 108, 103, 89, 19, 54, 113, 118, 68, 99, 104, 94, 83, 114, 109, 119, 84,
+    69,
+)
+SCATTER_PLAN = (
+    0, 0, 0, 0, 0, 0, 0, 0, 0, 0, 0, 0, 0, 0, 0, 1, 0, 0, 1, 0, 1, 1, 0, 1, 2, 1, 0, 0, 0, 1, 0, 0, 0, 1, 0, 0, 0, 0, 0, 3, 3, 3, 2,
+    2, 3, 2, 6, 1, 5, 0, 1, 1, 1, 7, 3, 0, 2, 8, 5,
+)
+
+
+def backward_kernel(count, chunks, modes, order, plan, slopes, table, refs_in, refs_out, scratch):
     (x_h, cot_h, a1_h, q_h, k_h, v_h, o_h, lse_h, x2_h, a2_h, u_h, gp_h, gdown_h, qkv_h, proj_h, up_h, down_h) = refs_in
     (layer_o, grad_o, gqkv_o, gproj_o, gup_o, gdown_o, sums_o) = refs_out
     landing = scratch[:count]
@@ -383,7 +412,7 @@
     t = lax.axis_index("tensor")
     other = 1 - t
     mine = bits_of(me, count)
-    orders = halving_orders(count)
+    orders = bit_orders(count, modes, len(chunks), False)
     tokens, model = cot.shape
     width = q_h.shape[1]
     hidden = gp.shape[1]
@@ -418,7 +447,7 @@
     size = chunks[0][3]
 
     def order_of(c):
-        return orders[SCATTER_MODES[c % len(SCATTER_MODES)]]
+        return orders[c]
 
     def held(c):
         name, lead, lo, _ = chunks[c]
@@ -445,7 +474,7 @@
                          device_id={"dp": partner_of(me, mine, order_of(c)[s])})
 
     def run(item):
-        at, c, s = item
+        c, s = item
         name, lead, lo, _ = chunks[c]
         copy_of(c, s - 1).wait_recv()
         got = landing[s - 1].at[c]
@@ -471,29 +500,30 @@
         lax.fori_loop(0, 1 << left, add, 0)
         copy_of(c, s).start()
 
-    queue = []
-    clock = [times["lead"]]
-    slot = [0.0]
-    each = times["scatter"] / len(chunks)
+    queue = [(code // (count + 1), code % (count + 1)) for code in order] if order and count == 4 else sorted(
+        ((c, s) for c in range(len(chunks)) for s in range(1, count + 1)), key=lambda cs: (cs[0] + LOOK * cs[1], cs[0]))
+    share = list(plan) if plan and count == 4 else []
+    open_chunks = set()
 
     def ready(names):
         for c, (name, lead, lo, _) in enumerate(chunks):
             if (name, lead, lo) in names:
-                slot[0] = max(clock[0], slot[0] + each)
                 copy_of(c, 0).start()
-                queue.extend((slot[0] + s * times["step"], c, s) for s in range(1, count + 1))
-        queue.sort()
+                open_chunks.add(c)
 
     def due():
         batch = []
-        while queue and queue[0][0] <= clock[0]:
-            batch.append(queue.pop(0))
+        for _ in range(share.pop(0) if share else 2):
+            if queue and queue[0][0] in open_chunks:
+                batch.append(queue.pop(0))
         return batch
 
-    def advance(cost):
-        clock[0] += cost
+    def advance():
         for item in due():
             run(item)
+
+    def paced(steps, body):
+        paced_loop(steps, body, [due() for _ in range(steps)], run)
 
     tiles = lambda name, total, lead=None, at=0: {(name, lead, lo) for lo in range(at, at + total, size)}
     ready(tiles("down", hidden))
@@ -502,7 +532,7 @@
     pos[...] = lax.broadcasted_iota(jnp.int32, pos.shape, 0).astype(F32)
 
     def whole(ref, h=None, cols=slice(None)):
-        return ref[:, cols] if h is None else ref[h * (model // 2) : (h + 1) * (model // 2), cols]
+        return ref[:, cols] if h is None else ref[span(h, model // 2), cols]
 
     loads["u"].wait()
     loads["down"].wait()
@@ -511,11 +541,12 @@
     def lowered(who, h):
         return dot_nt(big[who].reshape(local, hidden), whole(wide, h))
 
-    for h in range(2):
-        part[0:local, h * half : (h + 1) * half] = lowered(other, h).astype(BF)
+    def partner_lowered(h):
+        part[0:local, span(h, half)] = lowered(other, h).astype(BF)
+
+    paced(2, partner_lowered)
     first = mesh_copy(part.at[pl.ds(0, local)], first_r, psend.at[0], precv.at[0], device_id={"tensor": other})
     first.start()
-    advance(times["half"])
 
     loads["cot"].wait()
     loads["gp"].wait()
@@ -529,16 +560,17 @@
             at = slice(cols.start % model, cols.start % model + TILE)
             sums[0, line : line + 1, at] += jnp.sum(value.astype(F32), axis=0, keepdims=True)
 
-        rows_loop(tokens, 256, grad_pre)
-        advance(times["quarter"])
+        paced(tokens // 256, lambda i: grad_pre(i, span(i, 256)))
 
     loads["x2"].wait()
     first.wait_recv()
-    for h in range(2):
-        cols = slice(h * half, (h + 1) * half)
+
+    def own_lowered(h):
+        cols = span(h, half)
         mid = x2[rows_of(t, 0, local), cols]
         layer_o[:, cols] = (mid + (lowered(t, h) + first_r[:, cols].astype(F32)) + table[5:6, cols]).astype(BF)
-    advance(times["half"])
+
+    paced(2, own_lowered)
     load("qkv", qkv_h.at[0], wide.at[:, pl.ds(0, width)])
     load("qkv1", qkv_h.at[1], wide.at[:, pl.ds(width, width)])
     load("qkv2", qkv_h.at[2], wide.at[:, pl.ds(2 * width, width)])
@@ -550,21 +582,27 @@
     part_copies = []
     for h in range(2):
         rows = pl.ds(h * local, local)
-        for e in range(2):
-            part[rows, e * half : (e + 1) * half] = dot_nt(gp[rows, :], whole(up_w, e)).astype(BF)
+
+        def back_up(e, rows=rows):
+            part[rows, span(e, half)] = dot_nt(gp[rows, :], whole(up_w, e)).astype(BF)
+
+        paced(2, back_up)
         copy = mesh_copy(part.at[rows], part_r.at[rows], psend.at[1 + h], precv.at[1 + h], device_id={"tensor": other})
         copy.start()
         part_copies.append(copy)
-        advance(times["half"])
     for name, src, dst in (("q", q_h, q), ("k", k_h, k), ("v", v_h, v), ("o", o_h, o)):
         load(name, src, dst)
     for j in range(hidden // TILE):
         cols = slice(j * TILE, (j + 1) * TILE)
-        for h in range(2):
-            value = dot_tn(a1[:, h * half : (h + 1) * half], gp[:, cols]).astype(BF)
+
+        def sum_up(h, carry, cols=cols):
+            value = dot_tn(a1[:, span(h, half)], gp[:, cols]).astype(BF)
             big[(h, Ellipsis, cols)] = value.reshape(*big.shape[1:-1], TILE)
+            return carry
+
+        lax.fori_loop(0, 2, sum_up, 0)
         ready(tiles("up", TILE, at=j * TILE))
-        advance(times["quarter"])
+        advance()
     load("a1", a1_h, a1)
 
     def norm_parts(value):
@@ -583,7 +621,7 @@
         copy.wait_recv()
     for who, count_it in ((t, True), (other, False)):
 
-        def through(i, carry, who=who, count_it=count_it):
+        def through(i, who=who, count_it=count_it):
             rows = rows_of(who, i, 128)
             grad = part[rows, :].astype(F32) + part_r[rows, :].astype(F32)
             normed, inverse = norm_parts(x2[rows, :])
@@ -596,24 +634,26 @@
                 add_sum(3, mid)
                 add_sum(4, grad)
                 add_sum(5, outer)
-            return carry
-
-        lax.fori_loop(0, local // 128, through, 0)
-        advance(times["norm"])
+
+        paced(local // 128, through)
     gx2 = cot
 
     loads["proj"].wait()
     loads["o"].wait()
     proj_cols = slice(3 * width, 4 * width)
-    for h in range(2):
-        gproj[h] = dot_tn(gx2[:, h * half : (h + 1) * half], o[...]).astype(BF).reshape(gproj.shape[1:])
+
+    def sum_proj(h, carry):
+        gproj[h] = dot_tn(gx2[:, span(h, half)], o[...]).astype(BF).reshape(gproj.shape[1:])
+        return carry
+
+    lax.fori_loop(0, 2, sum_proj, 0)
     ready(tiles("proj", width))
-    advance(times["small"])
+    advance()
 
     def through_proj(i, rows):
         do[rows, :] = dot_nn(gx2[rows, :], whole(wide, cols=proj_cols)).astype(BF)
 
-    rows_loop(tokens, TILE, through_proj)
+    paced(tokens // TILE, lambda i: through_proj(i, span(i, TILE)))
     for name in ("q", "k", "v", "lse"):
         loads[name].wait()
 
@@ -621,24 +661,11 @@
         kt[:, rows] = k[rows, :].astype(F32).T.astype(BF)
 
     rows_loop(tokens, TILE, turn_keys)
-    advance(times["small"])
 
     blocks = tokens // QB
     lane_half = lax.broadcasted_iota(jnp.int32, (QB, 2 * HD), 1) // HD
-    batches = []
-    for h in range(heads):
-        batches.append(due())
-        clock[0] += times["head"]
-
-    def head_step(h, carry):
-        for j in range(heads):
-            if batches[j]:
-
-                @pl.when(h == j)
-                def _():
-                    for item in batches[j]:
-                        run(item)
-
+
+    def head_step(h):
         cols = span(h // 2, 2 * HD)
         head_rows = span(h, HD)
         side = lax.rem(h, 2)
@@ -674,9 +701,7 @@
             dk[:, cols] = acc_k[...].astype(BF)
             dv[:, cols] = acc_v[...].astype(BF)
 
-        return carry
-
-    lax.fori_loop(0, heads, head_step, 0)
+    paced(heads, head_step)
 
     def turn(i, rows):
         dq[rows, :] = dqt[:, rows].astype(F32).T.astype(BF)
@@ -684,10 +709,14 @@
     rows_loop(tokens, TILE, turn)
     loads["a1"].wait()
     for c, ref in ((1, dk), (2, dv), (0, dq)):
-        for h in range(2):
-            gqkv[c, h] = dot_tn(a1[:, h * half : (h + 1) * half], ref[...]).astype(BF).reshape(gqkv.shape[2:])
+
+        def sum_qkv(h, carry, c=c, ref=ref):
+            gqkv[c, h] = dot_tn(a1[:, span(h, half)], ref[...]).astype(BF).reshape(gqkv.shape[2:])
+            return carry
+
+        lax.fori_loop(0, 2, sum_qkv, 0)
         ready(tiles("qkv", width, lead=c))
-        advance(times["small"])
+        advance()
     for at, ref in ((0, dq), (width, dv)):
         sums[0, 10:11, at : at + width] = jnp.sum(ref[...].astype(F32), axis=0, keepdims=True)
 
@@ -702,18 +731,17 @@
     for copy in part_copies:
         copy.wait_send()
 
-    def partner_rows(i, carry):
+    def partner_rows(i):
         part[span(i, 256), :] = back_one(rows_of(other, i, 256)).astype(BF)
-        return carry
-
-    lax.fori_loop(0, local // 256, partner_rows, 0)
+
+    paced(local // 256, partner_rows)
     last = mesh_copy(part.at[pl.ds(0, local)], last_r, psend.at[3], precv.at[3], device_id={"tensor": other})
     last.start()
-    advance(times["half"])
+    advance()
     loads["x"].wait()
     last.wait_recv()
 
-    def own_rows(i, carry):
+    def own_rows(i):
         rows = rows_of(t, i, 256)
         here = span(i, 256)
         grad = back_one(rows) + last_r[here, :].astype(F32)
@@ -721,10 +749,8 @@
         grad_o[here, :] = x2[rows, :] + norm_back(grad, normed, inverse, table[0:1, :])
         add_sum(0, grad * normed)
         add_sum(2, grad)
-        return carry
-
-    lax.fori_loop(0, local // 256, own_rows, 0)
-    advance(times["half"])
+
+    paced(local // 256, own_rows)
 
     def sum_step(s):
         to = {"dp": partner_of(me, mine, s)} if s < count else {"tensor": other}
@@ -733,7 +759,7 @@
     sum_copies = [sum_step(s) for s in range(count + 1)]
     sum_copies[0].start()
     for s in range(count):
-        advance(times["hop"])
+        advance()
         sum_copies[s].wait_recv()
         sums[s + 1] = sums[s] + sland[s]
         sum_copies[s + 1].start()
@@ -749,10 +775,7 @@
         copy.wait_send()
 
 
-BACK_TIMES = {"scatter": 110.0, "step": 13.0, "lead": 3.0, "half": 3.0, "quarter": 1.7, "norm": 2.5, "small": 2.0, "head": 4.0, "hop": 2.5}
-
-
-def backward_all(slopes, table, x, cot, a1, q, k, v, o, lse, x2, a2, u, gp, gdown, qkv_w, proj_w, up_w, down_w, n, width=256, times=BACK_TIMES):
+def backward_all(slopes, table, x, cot, a1, q, k, v, o, lse, x2, a2, u, gp, gdown, qkv_w, proj_w, up_w, down_w, n, width=256):
     count = n.bit_length() - 1
     two = (2,) * count
     tokens, model = cot.shape
@@ -780,12 +803,34 @@
     by_block = lambda a: a.reshape(*two, r, a.shape[-1])
 
     def body(slopes_ref, table_ref, *refs):
-        backward_kernel(count, chunks, times, slopes_ref, table_ref, refs[:17], refs[17 : 17 + len(outs)], refs[17 + len(outs) :])
+        backward_kernel(count, chunks, SCATTER_MODES, SCATTER_ORDER, SCATTER_PLAN, slopes_ref, table_ref, refs[:17], refs[17 : 17 + len(outs)], refs[17 + len(outs) :])
 
     return pl.pallas_call(
         body, out_shape=outs, in_specs=[pl.BlockSpec(memory_space=pltpu.SMEM), VM] + [ANY] * 17, out_specs=[VM] * len(outs), scratch_shapes=scratch,
         compiler_params=pltpu.CompilerParams(collective_id=1, has_side_effects=True, vmem_limit_bytes=67043328), name="backward_all",
     )(slopes, table, x, cot, a1, q, k, v, o, lse, x2, a2, by_block(u), gp, by_block(gdown), flat(qkv_w), flat(proj_w), flat(up_w), flat(down_w))
+
+def finish_kernel(count, *refs):
+    ins, outs, bufs = refs[:count], refs[count : 2 * count], refs[2 * count : 3 * count]
+    in_sem, out_sem = refs[3 * count :]
+    reads = [pltpu.make_async_copy(a, b, in_sem.at[i]) for i, (a, b) in enumerate(zip(ins, bufs))]
+    writes = [pltpu.make_async_copy(b, c, out_sem.at[i]) for i, (b, c) in enumerate(zip(bufs, outs))]
+    for copy in reads:
+        copy.start()
+    for read, write in zip(reads, writes):
+        read.wait()
+        write.start()
+    for copy in writes:
+        copy.wait()
+
+
+def finish(arrays):
+    count = len(arrays)
+    return pl.pallas_call(
+        functools.partial(finish_kernel, count), out_shape=tuple(jax.ShapeDtypeStruct(a.shape, a.dtype) for a in arrays),
+        in_specs=[ANY] * count, out_specs=[ANY] * count,
+        scratch_shapes=[pltpu.VMEM(a.shape, a.dtype) for a in arrays] + [pltpu.SemaphoreType.DMA((count,))] * 2, name="finish")(*arrays)
+
 
 def on_device(layer_in, w_qkv, b_qv, w_proj, w_ff1, b_ff1, w_ff2, norm_gains, add_biases, cotangent):
     n = lax.axis_size("dp")
@@ -810,6 +855,8 @@
         slopes, w_qkv, w_proj.T, w_ff1, w_ff2.T, small, layer_in, cotangent, n)
     layer_out, grad_in, out_qkv, out_proj, out_up, out_down, sums = backward_all(
         slopes, vectors, layer_in, cot, a1, q, k, v, o, lse, x2, a2, u, rise, grad_down, qkv_w, proj_w, up_w, down_w, n)
+    layer_out, grad_in, out_qkv, out_proj, out_up, out_down, sums = finish(
+        (layer_out, grad_in, out_qkv, out_proj, out_up, out_down, sums))
     own = lax.dynamic_slice(sums, (zero, (2 * i + t) * part), (6, part))
     up_sums = lax.dynamic_slice_in_dim(sums[8 : 8 + hidden // model].reshape(up_grid), i * b_ff1.shape[1], b_ff1.shape[1], 1)
     qv_sums = lax.dynamic_slice_in_dim(sums[10].reshape(qv_grid), i * b_qv.shape[2], b_qv.shape[2], 2)

time: 304 us -> 254 us (0.84); the launches traced: 298 us -> 254 us
  Pallas kernels: 279 us -> 243 us
  local copies, waits for them, and re-layouts: 16.2 us -> 7.63 us
    pallas_call x1, Pallas kernels: 134 us -> 114 us  [forward_all(): pl.pallas_call(body, out_shape=tuple((jax.ShapeDtypeStruct(*s) for s in s...]
    pallas_call x1, Pallas kernels: 145 us -> 126 us  [backward_all(): pl.pallas_call(body, out_shape=outs, in_specs=[pl.BlockSpec(memory_space=...]
    unnamed x16 -> x2, local copies, waits for them, and re-layouts: 9.81 us -> 1.33 us
    pallas_call x0 -> x1, Pallas kernels: none -> 3.87 us  [finish(): pl.pallas_call(functools.partial(finish_kernel, count), out_shape=tuple((...]
where the time goes in v1:
time: 254 us
  Pallas kernels  243 us (96%)
  local copies, waits for them, and re-layouts  7.63 us (3%)
    pallas_call x1, Pallas kernels, backward_all(): pl.pallas_call(body, out_shape=outs, in_specs=[pl.BlockSpec(memory_space=...  126 us
    pallas_call x1, Pallas kernels, forward_all(): pl.pallas_call(body, out_shape=tuple((jax.ShapeDtypeStruct(*s) for s in s...  114 us

profile of v1, /device:TPU:0, one launch (start us, length us, event | category | flops | bytes accessed | tf_op | source)
XLA Modules:
  0.0 253.7 jit_solution(7700278153082061802)
XLA Ops:
  0.6 0.5 multiply_power_fusion.slopes_ref
  1.2 0.1 pad.3.clone
  1.3 0.7 pad_maximum_fusion
  2.0 0.8 copy.21
  2.7 0.1 dynamic_update_slice.11
  2.9 0.1 reshape.48
  2.9 0.8 copy.20
  3.7 0.2 dynamic_update_slice.10
  3.9 0.1 reshape.47
  4.0 0.4 dynamic_update_slice.9
  4.5 0.7 maximum_maximum_fusion.refs_4_
  5.2 113.6 %forward_all.1 = (bf16[3,2,2,2,2,64,512]{6,5,4,3,2,1,0:T(8,128)(2,1)}, bf16[2,2,2,2,64,512]{5,4,3,2,1,0:T(8,128)(2,1)}, bf16[2,2,2,2,64,2048]{5,4,3,2,1,0:T(8,12...) custom-call(f32[8]{0:T(128)} %multiply_power_fusion.slopes_ref, ...), custom_call_target="tpu_custom_call" | custom-call | tf_op jit(solution)/shard_map/forward_all/pallas_call | solution.py:383
  118.7 126.0 %backward_all.1 = (bf16[512,1024]{1,0:T(8,128)(2,1)}, f32[512,1024]{1,0:T(8,128)}, f32[3,64,512]{2,1,0:T(8,128)}, f32[64,512]{1,0:T(8,128)}, f32[64,2048]{1,0:T(...) custom-call(f32[8]{0:T(128)} %multiply_power_fusion.slopes_ref, f32[16,1024]{1,0:T(8,128)} %get-tuple-element.41.table_ref, ...), custom_call_target="tpu_custom_call" | custom-call | tf_op jit(solution)/shard_map/backward_all/pallas_call | solution.py:808
  244.7 3.9 %finish.1 = (bf16[512,1024]{1,0:T(8,128)(2,1)}, f32[512,1024]{1,0:T(8,128)}, f32[3,64,512]{2,1,0:T(8,128)}, f32[64,512]{1,0:T(8,128)}, f32[64,2048]{1,0:T(8,128)...) custom-call(bf16[512,1024]{1,0:T(8,128)(2,1)} %get-tuple-element.58.refs_0_, f32[512,1024]{1,0:T(8,128)} %get-tuple-element.59.refs_1_, ...), custom_call_target="tpu_custom_call" | custom-call | tf_op jit(solution)/shard_map/finish/pallas_call | solution.py:829
  248.6 0.8 constant_dynamic-slice_fusion
  249.3 0.6 slice.14
  249.9 0.6 slice.15
  250.5 0.8 slice_reduce_fusion
  251.3 0.8 slice.13
  252.1 0.1 constant_dynamic-slice_fusion.2
  252.2 0.7 copy.24
  252.8 0.1 reshape.55
  252.9 0.1 constant_dynamic-slice_fusion.1
  253.0 0.7 copy.25
  (5 shorter events, 0.1 us)

commit v2 on v1

--- a/solution.py
+++ b/solution.py
@@ -387,18 +387,18 @@
     )(slopes, qkv, proj, up, down, small, x, cot)
 
 SCATTER_MODES = (
-    123, 3012, 321, 213, 2310, 1203, 321, 1230, 2031, 1023, 132, 1032, 321, 1302, 1230, 231, 3102, 1023, 1032, 2013, 1032, 123, 1023,
-    213,
+    1023, 2013, 231, 1320, 1023, 3021, 213, 3012, 1320, 213, 213, 3021, 1203, 1023, 1302, 1023, 132, 213, 132, 1032, 3120, 213, 1023,
+    2013,
 )
 SCATTER_ORDER = (
-    1, 26, 11, 36, 2, 21, 27, 12, 37, 3, 46, 28, 6, 22, 41, 51, 56, 13, 31, 61, 16, 38, 4, 76, 7, 29, 71, 17, 47, 42, 23, 86, 57, 32,
-    39, 87, 77, 72, 52, 14, 62, 24, 33, 106, 48, 81, 91, 43, 8, 58, 96, 101, 66, 18, 116, 34, 111, 92, 73, 53, 78, 88, 97, 63, 102,
-    107, 9, 82, 112, 44, 59, 98, 74, 49, 79, 117, 64, 67, 93, 108, 103, 89, 19, 54, 113, 118, 68, 99, 104, 94, 83, 114, 109, 119, 84,
-    69,
+    1, 11, 26, 31, 16, 21, 2, 27, 22, 12, 32, 46, 3, 61, 17, 28, 23, 81, 41, 56, 51, 66, 36, 47, 62, 86, 13, 18, 71, 76, 4, 24, 29,
+    57, 67, 33, 96, 52, 82, 91, 37, 63, 6, 87, 42, 101, 106, 77, 19, 48, 68, 111, 14, 116, 97, 53, 92, 83, 7, 58, 38, 88, 34, 72, 112,
+    107, 64, 102, 117, 43, 8, 59, 78, 49, 73, 108, 98, 118, 69, 84, 93, 44, 54, 89, 113, 103, 39, 99, 109, 119, 94, 74, 79, 104, 114,
+    9,
 )
 SCATTER_PLAN = (
-    0, 0, 0, 0, 0, 0, 0, 0, 0, 0, 0, 0, 0, 0, 0, 1, 0, 0, 1, 0, 1, 1, 0, 1, 2, 1, 0, 0, 0, 1, 0, 0, 0, 1, 0, 0, 0, 0, 0, 3, 3, 3, 2,
-    2, 3, 2, 6, 1, 5, 0, 1, 1, 1, 7, 3, 0, 2, 8, 5,
+    0, 0, 0, 0, 0, 0, 0, 0, 0, 0, 0, 0, 0, 0, 0, 0, 0, 0, 0, 2, 0, 1, 2, 1, 1, 1, 1, 0, 0, 1, 0, 0, 0, 0, 0, 0, 1, 0, 0, 1, 3, 2, 4,
+    1, 4, 5, 5, 5, 0, 1, 4, 4, 3, 3, 4, 7, 6,
 )
 
 
@@ -505,11 +505,13 @@
     share = list(plan) if plan and count == 4 else []
     open_chunks = set()
 
-    def ready(names):
+    def ready(names, mark=True, start=True):
         for c, (name, lead, lo, _) in enumerate(chunks):
             if (name, lead, lo) in names:
-                copy_of(c, 0).start()
-                open_chunks.add(c)
+                if start:
+                    copy_of(c, 0).start()
+                if mark:
+                    open_chunks.add(c)
 
     def due():
         batch = []
@@ -665,7 +667,32 @@
     blocks = tokens // QB
     lane_half = lax.broadcasted_iota(jnp.int32, (QB, 2 * HD), 1) // HD
 
+    group = width // 2
+
+    def group_names(g):
+        return {("qkv", c, lo) for c in range(3) for lo in range(g * group, (g + 1) * group, size)}
+
+    def group_grads(g):
+        cols = slice(g * group, (g + 1) * group)
+
+        def turn(i, rows):
+            dq[rows, cols] = dqt[cols, rows].astype(F32).T.astype(BF)
+
+        rows_loop(tokens, TILE, turn)
+        for c, ref in ((1, dk), (2, dv), (0, dq)):
+
+            def sum_qkv(h, carry, c=c, ref=ref):
+                gqkv[(c, h, Ellipsis, cols)] = dot_tn(a1[:, span(h, half)], ref[:, cols]).astype(BF).reshape(*gqkv.shape[2:-1], group)
+                return carry
+
+            lax.fori_loop(0, 2, sum_qkv, 0)
+
     def head_step(h):
+        @pl.when(h == heads // 2)
+        def _():
+            group_grads(0)
+            ready(group_names(0), mark=False)
+
         cols = span(h // 2, 2 * HD)
         head_rows = span(h, HD)
         side = lax.rem(h, 2)
@@ -701,22 +728,13 @@
             dk[:, cols] = acc_k[...].astype(BF)
             dv[:, cols] = acc_v[...].astype(BF)
 
-    paced(heads, head_step)
-
-    def turn(i, rows):
-        dq[rows, :] = dqt[:, rows].astype(F32).T.astype(BF)
-
-    rows_loop(tokens, TILE, turn)
     loads["a1"].wait()
-    for c, ref in ((1, dk), (2, dv), (0, dq)):
-
-        def sum_qkv(h, carry, c=c, ref=ref):
-            gqkv[c, h] = dot_tn(a1[:, span(h, half)], ref[...]).astype(BF).reshape(gqkv.shape[2:])
-            return carry
-
-        lax.fori_loop(0, 2, sum_qkv, 0)
-        ready(tiles("qkv", width, lead=c))
-        advance()
+    batches = [due() for _ in range(heads // 2 + 1)]
+    ready(group_names(0), start=False)
+    paced_loop(heads, head_step, batches + [due() for _ in range(heads // 2 - 1)], run)
+    group_grads(1)
+    ready(group_names(1))
+    advance()
     for at, ref in ((0, dq), (width, dv)):
         sums[0, 10:11, at : at + width] = jnp.sum(ref[...].astype(F32), axis=0, keepdims=True)
 
@@ -785,8 +803,7 @@
     chunks = [("down", None, lo, width) for lo in range(0, hidden, width)]
     chunks += [("up", None, lo, width) for lo in range(0, hidden, width)]
     chunks += [("proj", None, lo, width) for lo in range(0, inner, width)]
-    for c in (1, 2, 0):
-        chunks += [("qkv", c, lo, width) for lo in range(0, inner, width)]
+    chunks += [("qkv", c, lo, width) for lo in range(0, inner, width) for c in (1, 2, 0)]
     f = lambda *s: jax.ShapeDtypeStruct(s, F32)
     outs = (jax.ShapeDtypeStruct(x.shape, BF), f(*x.shape), f(3, r, inner), f(r, inner), f(r, hidden), f(r, hidden), f(16, model))
     vm = lambda *s, d=BF: pltpu.VMEM(s, d)

time: 254 us -> 241 us (0.949)
  Pallas kernels: 243 us -> 231 us
    pallas_call x1, Pallas kernels: 126 us -> 113 us  [backward_all(): pl.pallas_call(body, out_shape=outs, in_specs=[pl.BlockSpec(memory_space=...]
where the time goes in v2:
time: 241 us
  Pallas kernels  231 us (96%)
  local copies, waits for them, and re-layouts  7.63 us (3%)
    pallas_call x1, Pallas kernels, forward_all(): pl.pallas_call(body, out_shape=tuple((jax.ShapeDtypeStruct(*s) for s in s...  114 us
    pallas_call x1, Pallas kernels, backward_all(): pl.pallas_call(body, out_shape=outs, in_specs=[pl.BlockSpec(memory_space=...  113 us

profile of v2, /device:TPU:0, one launch (start us, length us, event | category | flops | bytes accessed | tf_op | source)
XLA Modules:
  0.0 240.9 jit_solution(16399364532650137780)
XLA Ops:
  0.6 0.5 multiply_power_fusion.slopes_ref
  1.2 0.1 pad.3.clone
  1.3 0.7 pad_maximum_fusion
  2.0 0.8 copy.21
  2.7 0.1 dynamic_update_slice.11
  2.9 0.1 reshape.48
  2.9 0.8 copy.20
  3.7 0.2 dynamic_update_slice.10
  3.9 0.1 reshape.47
  4.0 0.4 dynamic_update_slice.9
  4.5 0.7 maximum_maximum_fusion.refs_4_
  5.2 113.6 %forward_all.1 = (bf16[3,2,2,2,2,64,512]{6,5,4,3,2,1,0:T(8,128)(2,1)}, bf16[2,2,2,2,64,512]{5,4,3,2,1,0:T(8,128)(2,1)}, bf16[2,2,2,2,64,2048]{5,4,3,2,1,0:T(8,12...) custom-call(f32[8]{0:T(128)} %multiply_power_fusion.slopes_ref, ...), custom_call_target="tpu_custom_call" | custom-call | tf_op jit(solution)/shard_map/forward_all/pallas_call | solution.py:383
  118.7 113.2 %backward_all.1 = (bf16[512,1024]{1,0:T(8,128)(2,1)}, f32[512,1024]{1,0:T(8,128)}, f32[3,64,512]{2,1,0:T(8,128)}, f32[64,512]{1,0:T(8,128)}, f32[64,2048]{1,0:T(...) custom-call(f32[8]{0:T(128)} %multiply_power_fusion.slopes_ref, f32[16,1024]{1,0:T(8,128)} %get-tuple-element.41.table_ref, ...), custom_call_target="tpu_custom_call" | custom-call | tf_op jit(solution)/shard_map/backward_all/pallas_call | solution.py:825
  231.9 3.9 %finish.1 = (bf16[512,1024]{1,0:T(8,128)(2,1)}, f32[512,1024]{1,0:T(8,128)}, f32[3,64,512]{2,1,0:T(8,128)}, f32[64,512]{1,0:T(8,128)}, f32[64,2048]{1,0:T(8,128)...) custom-call(bf16[512,1024]{1,0:T(8,128)(2,1)} %get-tuple-element.58.refs_0_, f32[512,1024]{1,0:T(8,128)} %get-tuple-element.59.refs_1_, ...), custom_call_target="tpu_custom_call" | custom-call | tf_op jit(solution)/shard_map/finish/pallas_call | solution.py:846
  235.8 0.8 constant_dynamic-slice_fusion
  236.6 0.6 slice.14
  237.2 0.6 slice.15
  237.7 0.8 slice_reduce_fusion
  238.5 0.8 slice.13
  239.3 0.1 constant_dynamic-slice_fusion.2
  239.4 0.7 copy.24
  240.1 0.1 reshape.55
  240.2 0.1 constant_dynamic-slice_fusion.1
  240.2 0.7 copy.25
  (5 shorter events, 0.1 us)

commit v3 on v2

--- a/solution.py
+++ b/solution.py
@@ -828,8 +828,8 @@
     )(slopes, table, x, cot, a1, q, k, v, o, lse, x2, a2, by_block(u), gp, by_block(gdown), flat(qkv_w), flat(proj_w), flat(up_w), flat(down_w))
 
 def finish_kernel(count, *refs):
-    ins, outs, bufs = refs[:count], refs[count : 2 * count], refs[2 * count : 3 * count]
-    in_sem, out_sem = refs[3 * count :]
+    ins, outs, refs = refs[:count], refs[count : 2 * count], refs[2 * count :]
+    gains_o, shifts_o, bufs, (in_sem, out_sem) = refs[0], refs[1], refs[2 : 2 + count], refs[2 + count :]
     reads = [pltpu.make_async_copy(a, b, in_sem.at[i]) for i, (a, b) in enumerate(zip(ins, bufs))]
     writes = [pltpu.make_async_copy(b, c, out_sem.at[i]) for i, (b, c) in enumerate(zip(bufs, outs))]
     for copy in reads:
@@ -837,15 +837,22 @@
     for read, write in zip(reads, writes):
         read.wait()
         write.start()
+    part = gains_o.shape[1]
+    base = (2 * lax.axis_index("dp") + lax.axis_index("tensor")) * part
+    block = bufs[-1][0:8, span(base // 128, 128)]
+    turned = pltpu.roll(block, lax.rem(128 - lax.rem(base, 128), 128), 1)
+    gains_o[...] = turned[0:2, 0:part]
+    shifts_o[...] = turned[2:6, 0:part]
     for copy in writes:
         copy.wait()
 
 
-def finish(arrays):
+def finish(arrays, part):
     count = len(arrays)
+    vectors = (jax.ShapeDtypeStruct((2, part), F32), jax.ShapeDtypeStruct((4, part), F32))
     return pl.pallas_call(
-        functools.partial(finish_kernel, count), out_shape=tuple(jax.ShapeDtypeStruct(a.shape, a.dtype) for a in arrays),
-        in_specs=[ANY] * count, out_specs=[ANY] * count,
+        functools.partial(finish_kernel, count), out_shape=tuple(jax.ShapeDtypeStruct(a.shape, a.dtype) for a in arrays) + vectors,
+        in_specs=[ANY] * count, out_specs=[ANY] * count + [VM] * 2,
         scratch_shapes=[pltpu.VMEM(a.shape, a.dtype) for a in arrays] + [pltpu.SemaphoreType.DMA((count,))] * 2, name="finish")(*arrays)
 
 
@@ -872,12 +879,11 @@
         slopes, w_qkv, w_proj.T, w_ff1, w_ff2.T, small, layer_in, cotangent, n)
     layer_out, grad_in, out_qkv, out_proj, out_up, out_down, sums = backward_all(
         slopes, vectors, layer_in, cot, a1, q, k, v, o, lse, x2, a2, u, rise, grad_down, qkv_w, proj_w, up_w, down_w, n)
-    layer_out, grad_in, out_qkv, out_proj, out_up, out_down, sums = finish(
-        (layer_out, grad_in, out_qkv, out_proj, out_up, out_down, sums))
-    own = lax.dynamic_slice(sums, (zero, (2 * i + t) * part), (6, part))
+    layer_out, grad_in, out_qkv, out_proj, out_up, out_down, sums, out_gains, out_shifts = finish(
+        (layer_out, grad_in, out_qkv, out_proj, out_up, out_down, sums), part)
     up_sums = lax.dynamic_slice_in_dim(sums[8 : 8 + hidden // model].reshape(up_grid), i * b_ff1.shape[1], b_ff1.shape[1], 1)
     qv_sums = lax.dynamic_slice_in_dim(sums[10].reshape(qv_grid), i * b_qv.shape[2], b_qv.shape[2], 2)
-    return (layer_out, grad_in, out_qkv, qv_sums, out_proj.T, out_up, up_sums, out_down.T, own[:2], own[2:])
+    return (layer_out, grad_in, out_qkv, qv_sums, out_proj.T, out_up, up_sums, out_down.T, out_gains, out_shifts)
 
 
 def solution(mesh):

time: 241 us -> 240 us (level)
  no operation moved by 1% of the time
where the time goes in v3:
time: 240 us
  Pallas kernels  231 us (96%)
  local copies, waits for them, and re-layouts  5.72 us (2%)
    pallas_call x1, Pallas kernels, forward_all(): pl.pallas_call(body, out_shape=tuple((jax.ShapeDtypeStruct(*s) for s in s...  114 us
    pallas_call x1, Pallas kernels, backward_all(): pl.pallas_call(body, out_shape=outs, in_specs=[pl.BlockSpec(memory_space=...  113 us

profile of v3, /device:TPU:0, one launch (start us, length us, event | category | flops | bytes accessed | tf_op | source)
XLA Modules:
  0.0 239.6 jit_solution(8760801478458978220)
XLA Ops:
  0.6 0.5 multiply_power_fusion.slopes_ref
  1.2 0.1 pad.3.clone
  1.3 0.7 pad_maximum_fusion
  2.0 0.8 copy.21
  2.7 0.1 dynamic_update_slice.11
  2.9 0.1 reshape.48
  2.9 0.8 copy.20
  3.7 0.2 dynamic_update_slice.10
  3.9 0.1 reshape.47
  4.0 0.4 dynamic_update_slice.9
  4.5 0.7 maximum_maximum_fusion.refs_4_
  5.2 113.6 %forward_all.1 = (bf16[3,2,2,2,2,64,512]{6,5,4,3,2,1,0:T(8,128)(2,1)}, bf16[2,2,2,2,64,512]{5,4,3,2,1,0:T(8,128)(2,1)}, bf16[2,2,2,2,64,2048]{5,4,3,2,1,0:T(8,12...) custom-call(f32[8]{0:T(128)} %multiply_power_fusion.slopes_ref, ...), custom_call_target="tpu_custom_call" | custom-call | tf_op jit(solution)/shard_map/forward_all/pallas_call | solution.py:383
  118.7 113.2 %backward_all.1 = (bf16[512,1024]{1,0:T(8,128)(2,1)}, f32[512,1024]{1,0:T(8,128)}, f32[3,64,512]{2,1,0:T(8,128)}, f32[64,512]{1,0:T(8,128)}, f32[64,2048]{1,0:T(...) custom-call(f32[8]{0:T(128)} %multiply_power_fusion.slopes_ref, f32[16,1024]{1,0:T(8,128)} %get-tuple-element.43.table_ref, ...), custom_call_target="tpu_custom_call" | custom-call | tf_op jit(solution)/shard_map/backward_all/pallas_call | solution.py:825
  231.9 4.5 %finish.1 = (bf16[512,1024]{1,0:T(8,128)(2,1)}, f32[512,1024]{1,0:T(8,128)}, f32[3,64,512]{2,1,0:T(8,128)}, f32[64,512]{1,0:T(8,128)}, f32[64,2048]{1,0:T(8,128)...) custom-call(bf16[512,1024]{1,0:T(8,128)(2,1)} %get-tuple-element.60.refs_0_, ...), custom_call_target="tpu_custom_call" | custom-call | tf_op jit(solution)/shard_map/finish/pallas_call | solution.py:853
  236.4 0.8 slice_reduce_fusion
  237.2 0.8 slice.7
  237.9 0.1 reshape_squeeze.3
  238.0 0.1 constant_dynamic-slice_fusion.1
  238.1 0.7 copy.24
  238.8 0.1 reshape.55
  238.9 0.1 constant_dynamic-slice_fusion
  238.9 0.7 copy.25
  (4 shorter events, 0.0 us)

commit v4 on v3

--- a/solution.py
+++ b/solution.py
@@ -339,16 +339,16 @@
 
 
 GATHER_MODES = (
-    3201, 1320, 3210, 2130, 2301, 3201, 3021, 1320, 3021, 3201, 3021, 1230, 2310, 3012, 3201, 1230, 3120, 2031, 1032, 2031, 321, 1230,
-    3210, 213,
+    3021, 2130, 2031, 3210, 3120, 2301, 3210, 1320, 3201, 3210, 2301, 3210, 1320, 1203, 1302, 3012, 312, 1320, 231, 3201, 2310, 2031,
+    2031, 321,
 )
 GATHER_ORDER = (
-    16, 8, 20, 68, 17, 12, 9, 69, 40, 4, 21, 13, 0, 5, 70, 10, 18, 48, 36, 41, 14, 22, 84, 1, 28, 11, 19, 24, 6, 85, 42, 29, 49, 23,
-    32, 71, 44, 2, 37, 52, 64, 60, 7, 3, 86, 15, 25, 43, 30, 56, 76, 45, 88, 61, 38, 50, 92, 33, 53, 72, 65, 26, 31, 80, 39, 77, 93,
-    46, 87, 34, 57, 54, 62, 89, 51, 73, 27, 66, 94, 81, 78, 47, 35, 58, 55, 63, 90, 67, 74, 82, 95, 79, 59, 91, 75, 83,
+    20, 36, 12, 4, 0, 21, 37, 8, 5, 13, 92, 32, 1, 16, 6, 38, 93, 9, 28, 22, 2, 14, 84, 33, 10, 17, 39, 24, 29, 44, 40, 23, 15, 7, 18,
+    3, 85, 94, 34, 60, 52, 76, 11, 48, 41, 25, 56, 53, 19, 30, 45, 72, 95, 86, 61, 64, 77, 80, 35, 49, 57, 26, 42, 68, 54, 88, 31, 73,
+    46, 62, 65, 87, 78, 43, 81, 50, 55, 27, 89, 58, 69, 74, 47, 66, 82, 63, 51, 79, 90, 70, 59, 67, 75, 83, 71, 91,
 )
 GATHER_PLAN = (
-    41, 2, 3, 2, 2, 7, 0, 1, 0, 4, 0, 0, 1, 2, 2, 0, 4, 3, 3, 2, 1, 2, 1, 5, 0, 3, 1, 0, 0, 0, 0, 0, 1, 0, 1, 0, 0, 0, 1, 0, 0, 1, 0,
+    39, 3, 2, 3, 3, 4, 2, 2, 0, 2, 3, 1, 1, 2, 1, 1, 2, 2, 2, 2, 4, 1, 3, 3, 1, 2, 0, 0, 0, 1, 0, 0, 0, 2, 0, 0, 0, 0, 0, 0, 0, 2, 0,
     0, 0, 0, 0, 0, 0, 0, 0, 0, 0,
 )
 

time: 240 us -> 238 us (level)
  no operation moved by 1% of the time
where the time goes in v4:
time: 238 us
  Pallas kernels  230 us (97%)
  local copies, waits for them, and re-layouts  5.72 us (2%)
    pallas_call x1, Pallas kernels, backward_all(): pl.pallas_call(body, out_shape=outs, in_specs=[pl.BlockSpec(memory_space=...  113 us
    pallas_call x1, Pallas kernels, forward_all(): pl.pallas_call(body, out_shape=tuple((jax.ShapeDtypeStruct(*s) for s in s...  112 us

profile of v4, /device:TPU:0, one launch (start us, length us, event | category | flops | bytes accessed | tf_op | source)
XLA Modules:
  0.0 238.0 jit_solution(18126928617891819950)
XLA Ops:
  0.6 0.5 multiply_power_fusion.slopes_ref
  1.2 0.1 pad.3.clone
  1.3 0.7 pad_maximum_fusion
  2.0 0.8 copy.21
  2.7 0.1 dynamic_update_slice.11
  2.9 0.1 reshape.48
  2.9 0.8 copy.20
  3.7 0.2 dynamic_update_slice.10
  3.9 0.1 reshape.47
  4.0 0.4 dynamic_update_slice.9
  4.5 0.7 maximum_maximum_fusion.refs_4_
  5.2 112.0 %forward_all.1 = (bf16[3,2,2,2,2,64,512]{6,5,4,3,2,1,0:T(8,128)(2,1)}, bf16[2,2,2,2,64,512]{5,4,3,2,1,0:T(8,128)(2,1)}, bf16[2,2,2,2,64,2048]{5,4,3,2,1,0:T(8,12...) custom-call(f32[8]{0:T(128)} %multiply_power_fusion.slopes_ref, ...), custom_call_target="tpu_custom_call" | custom-call | tf_op jit(solution)/shard_map/forward_all/pallas_call | solution.py:383
  117.2 113.2 %backward_all.1 = (bf16[512,1024]{1,0:T(8,128)(2,1)}, f32[512,1024]{1,0:T(8,128)}, f32[3,64,512]{2,1,0:T(8,128)}, f32[64,512]{1,0:T(8,128)}, f32[64,2048]{1,0:T(...) custom-call(f32[8]{0:T(128)} %multiply_power_fusion.slopes_ref, f32[16,1024]{1,0:T(8,128)} %get-tuple-element.43.table_ref, ...), custom_call_target="tpu_custom_call" | custom-call | tf_op jit(solution)/shard_map/backward_all/pallas_call | solution.py:825
  230.4 4.5 %finish.1 = (bf16[512,1024]{1,0:T(8,128)(2,1)}, f32[512,1024]{1,0:T(8,128)}, f32[3,64,512]{2,1,0:T(8,128)}, f32[64,512]{1,0:T(8,128)}, f32[64,2048]{1,0:T(8,128)...) custom-call(bf16[512,1024]{1,0:T(8,128)(2,1)} %get-tuple-element.60.refs_0_, ...), custom_call_target="tpu_custom_call" | custom-call | tf_op jit(solution)/shard_map/finish/pallas_call | solution.py:853
  234.9 0.8 slice_reduce_fusion
  235.6 0.8 slice.7
  236.4 0.1 reshape_squeeze.3
  236.5 0.1 constant_dynamic-slice_fusion.1
  236.5 0.7 copy.24
  237.2 0.1 reshape.55
  237.3 0.1 constant_dynamic-slice_fusion
  237.4 0.7 copy.25
  (4 shorter events, 0.0 us)
